TPU v7x, 32 devices: a whole 2x2x4 slice. The times are simulated.
32 devices in a mesh: seq: 8 (over y, x, core), head: 4 (over z).
Axes of the slice: x: 2, y: 2, z: 4, core: 2. Of those that a mesh axis runs over, the one named last changes fastest.
Arguments:
- queries: bfloat16 [8192, 32, 128], P('seq', 'head'), may hold values from -6 to 6
- key_vectors: bfloat16 [8192, 32, 128], P('seq', 'head'), may hold values from -6 to 6
- value_vectors: bfloat16 [8192, 32, 128], P('seq', 'head'), may hold values from -6 to 6
- out_grad: bfloat16 [8192, 32, 128], P(('seq', 'head')), may hold values from -6 to 6
Outputs:
- attended: bfloat16 [8192, 32, 128], P(('seq', 'head'))
- query_grad: bfloat16 [8192, 32, 128], P('seq', 'head')
- key_grad: bfloat16 [8192, 32, 128], P('seq', 'head')
- value_grad: bfloat16 [8192, 32, 128], P('seq', 'head')
All inputs are finite; a program needn't handle non-finite values.
Results may differ from a plain program's by a relative error of at most 0.0058.
Values may be sent and summed in bfloat16 or wider, within the bound.
No kernel may reach another device: no remote copies, remote signals or barrier semaphores. Data moves between devices by JAX's collectives and lax.ppermute only.
A program may use at most 128 MiB of HBM per device.

v0:
```python
import jax
import jax.numpy as jnp
from jax import lax
from jax.sharding import PartitionSpec as P


def per_device(queries, key_vectors, value_vectors, out_grad):
    tok_rows, heads_local, head_size = queries.shape
    grad_full = lax.all_to_all(out_grad, "head", split_axis=1, concat_axis=0, tiled=True)
    position = (lax.axis_index("seq") * tok_rows + lax.iota(jnp.int32, tok_rows)).astype(
        jnp.float32
    )
    scaling = 1.0 / jnp.sqrt(head_size * (position + 1.0))
    scaled_grad = (scaling[:, None, None] * grad_full.astype(jnp.float32)).astype(jnp.bfloat16)
    seg_state = jnp.einsum(
        "shd,she->hde", key_vectors, value_vectors, preferred_element_type=jnp.float32
    )
    grad_state = jnp.einsum(
        "thd,the->hde", queries, scaled_grad, preferred_element_type=jnp.float32
    )
    pieces = (
        lax.all_gather(seg_state[None], "seq", axis=0, tiled=True),
        lax.all_gather(grad_state[None], "seq", axis=0, tiled=True),
    )
    piece_rows = pieces[0].shape[0]
    index_rows = lax.iota(jnp.int32, piece_rows)
    own_index = lax.axis_index("seq")
    below_mask = (index_rows < own_index).astype(jnp.float32)[:, None, None, None]
    above_mask = (index_rows > own_index).astype(jnp.float32)[:, None, None, None]
    prefix_sum = jnp.sum(below_mask * pieces[0], axis=0)
    suffix_sum = jnp.sum(above_mask * pieces[1], axis=0)
    prefix = prefix_sum.astype(jnp.bfloat16)
    suffix = suffix_sum.astype(jnp.bfloat16)
    block_rows = min(512, tok_rows)
    attended_blocks = []
    query_blocks = []
    key_accum = jnp.zeros((tok_rows, heads_local, head_size), jnp.float32)
    value_accum = jnp.zeros((tok_rows, heads_local, head_size), jnp.float32)
    for block_index in range(tok_rows // block_rows):
        row_start = block_index * block_rows
        row_end = row_start + block_rows
        query_block = queries[row_start:row_end]
        grad_block = scaled_grad[row_start:row_end]
        key_past = key_vectors[:row_end]
        value_past = value_vectors[:row_end]
        causal = (
            lax.iota(jnp.int32, row_end)[None, :]
            <= (row_start + lax.iota(jnp.int32, block_rows))[:, None]
        )[None]
        within = jnp.where(
            causal,
            jnp.einsum("thd,shd->hts", query_block, key_past, preferred_element_type=jnp.float32),
            0.0,
        ).astype(jnp.bfloat16)
        grad_scores = jnp.where(
            causal,
            jnp.einsum("thd,shd->hts", grad_block, value_past, preferred_element_type=jnp.float32),
            0.0,
        ).astype(jnp.bfloat16)
        carried = jnp.einsum(
            "thd,hde->the", query_block, prefix, preferred_element_type=jnp.float32
        )
        local_sum = jnp.einsum(
            "hts,shd->thd", within, value_past, preferred_element_type=jnp.float32
        )
        attended_blocks.append(
            (scaling[row_start:row_end, None, None] * (carried + local_sum)).astype(jnp.bfloat16)
        )
        query_part = jnp.einsum(
            "the,hde->thd", grad_block, prefix, preferred_element_type=jnp.float32
        )
        query_part = query_part + jnp.einsum(
            "hts,shd->thd", grad_scores, key_past, preferred_element_type=jnp.float32
        )
        query_blocks.append(query_part.astype(jnp.bfloat16))
        key_accum = key_accum.at[:row_end].add(
            jnp.einsum("hts,thd->shd", grad_scores, query_block, preferred_element_type=jnp.float32)
        )
        value_accum = value_accum.at[:row_end].add(
            jnp.einsum("hts,the->she", within, grad_block, preferred_element_type=jnp.float32)
        )
    key_grad = key_accum + jnp.einsum(
        "shj,hij->shi", value_vectors, suffix, preferred_element_type=jnp.float32
    )
    value_grad = value_accum + jnp.einsum(
        "shi,hij->shj", key_vectors, suffix, preferred_element_type=jnp.float32
    )
    attended_heads = jnp.concatenate(attended_blocks, axis=0)
    attended = lax.all_to_all(attended_heads, "head", split_axis=0, concat_axis=1, tiled=True)
    query_grad = jnp.concatenate(query_blocks, axis=0)
    return (attended, query_grad, key_grad.astype(jnp.bfloat16), value_grad.astype(jnp.bfloat16))


def solution(mesh):
    return jax.shard_map(
        per_device,
        mesh=mesh,
        in_specs=(
            P("seq", "head", None),
            P("seq", "head", None),
            P("seq", "head", None),
            P(("seq", "head"), None, None),
        ),
        out_specs=(
            P(("seq", "head"), None, None),
            P("seq", "head", None),
            P("seq", "head", None),
            P("seq", "head", None),
        ),
        check_vma=False,
    )
```

profile of v0, /device:TPU:0, one launch (start us, length us, event | category | flops | bytes accessed | tf_op | source)
XLA Modules:
  0.0 183.0 jit_solution(1215966537800625695)
XLA Ops:
  7.2 4.4 %fusion.34 = f32[8,128,128]{2,1,0:T(8,128)} fusion(bf16[1024,8,128]{2,1,0:T(8,128)(2,1)} %param.17, bf16[1024,8,128]{2,1,0:T(8,128)(2,1)} %param.18), kind=kOutput, calls=%fused_computation.61 | convolution fusion | flops 268435456 | bytes 4718592 | tf_op jit(solution)/shard_map/shd,she->hde/dot_general | solution.py:15
  11.7 2.1 %copy.87 = bf16[256,32,128]{2,0,1:T(8,128)(2,1)} copy(bf16[256,32,128]{2,1,0:T(8,128)(2,1)S(1)} %copy-done.22) | data formatting | bytes 4194304 | tf_op args[3]
  13.8 6.5 %all-to-all-start.1 = ((bf16[256,32,128]{2,0,1:T(8,128)(2,1)}), bf16[256,32,128]{2,0,1:T(8,128)(2,1)}, u32[]{:S(2)}, u32[]{:S(2)}) async-start(bf16[256,32,128]{2,0,1:T(8,128)(2,1)} %copy.87), calls=%async_computation.1 | async-start | bytes 4194304 | tf_op jit(solution)/shard_map/all_to_all | solution.py:9
  26.8 4.7 %select_convert_fusion.3 = bf16[8,512,512]{2,1,0:T(8,128)(2,1)} fusion(pred[512,512]{1,0:T(8,128)(4,1)S(1)} %iota_compare_fusion.1, bf16[1024,8,128]{2,0,1:T(8,128)(2,1)} %copy.77, bf16[1024,8,128]{2,0,1:T(8,128)(2,1)S(1)} %copy.75), kind=kOutput, calls=%fused_computation.3 | convolution fusion | flops 541065216 | bytes 6553600 | tf_op jit(solution)/shard_map/thd,shd->hts/dot_general | solution.py:52
  31.6 6.0 %select_convert_fusion.1 = bf16[8,512,1024]{2,1,0:T(8,128)(2,1)} fusion(pred[512,1024]{1,0:T(8,128)(4,1)S(1)} %iota_compare_fusion, bf16[1024,8,128]{2,0,1:T(8,128)(2,1)S(1)} %copy.75, bf16[1024,8,128]{2,1,0:T(8,128)(2,1)S(1)} %copy-done.17), kind=kOutput, calls=%fused_computation.1 | convolution fusion | flops 1082130432 | bytes 12058624 | tf_op jit(solution)/shard_map/thd,shd->hts/dot_general | solution.py:52
  37.6 31.1 %all-to-all-done.1 = bf16[256,32,128]{2,0,1:T(8,128)(2,1)} async-done(((bf16[256,32,128]{2,0,1:T(8,128)(2,1)}), bf16[256,32,128]{2,0,1:T(8,128)(2,1)}, u32[]{:S(2)}, u32[]{:S(2)}) %all-to-all-start.1) | async-done | bytes 2097184 | tf_op jit(solution)/shard_map/all_to_all | solution.py:9
  74.3 2.7 %select_convert_fusion.2 = bf16[8,512,512]{2,1,0:T(8,128)(2,1)S(1)} fusion(pred[512,512]{1,0:T(8,128)(4,1)S(1)} %iota_compare_fusion.1, bf16[1024,8,128]{2,0,1:T(8,128)(2,1)} %copy.74, bf16[1024,8,128]{2,0,1:T(8,128)(2,1)S(1)} %fusion), kind=kOutput, calls=%fused_computation.2 | convolution fusion | flops 541065216 | bytes 6553600 | tf_op jit(solution)/shard_map/thd,shd->hts/dot_general | solution.py:57
  77.0 2.8 %convolution_bitcast_fusion.1 = f32[512,8,128]{2,0,1:T(8,128)} fusion(bf16[8,512,512]{2,1,0:T(8,128)(2,1)S(1)} %select_convert_fusion.2, bf16[1024,8,128]{2,0,1:T(8,128)(2,1)S(1)} %copy-done.2), kind=kOutput, calls=%fused_computation.29 | convolution fusion | flops 536870912 | bytes 7340032 | tf_op jit(solution)/shard_map/hts,thd->shd/dot_general | solution.py:77
  81.5 2.2 %convolution_bitcast_fusion = f32[512,8,128]{0,2,1:T(8,128)} fusion(bf16[8,512,512]{2,1,0:T(8,128)(2,1)S(1)} %copy-done.4, bf16[1024,8,128]{2,0,1:T(8,128)(2,1)S(1)} %fusion), kind=kOutput, calls=%fused_computation.28 | convolution fusion | flops 536870912 | bytes 7340032 | tf_op jit(solution)/shard_map/hts,the->she/dot_general | solution.py:80
  83.8 2.7 %select_convert_fusion = bf16[8,512,1024]{2,1,0:T(8,128)(2,1)S(1)} fusion(pred[512,1024]{1,0:T(8,128)(4,1)S(1)} %iota_compare_fusion, bf16[1024,8,128]{2,0,1:T(8,128)(2,1)S(1)} %fusion, bf16[1024,8,128]{2,1,0:T(8,128)(2,1)S(1)} %copy-done.14), kind=kOutput, calls=%fused_computation | convolution fusion | flops 1082130432 | bytes 12058624 | tf_op jit(solution)/shard_map/thd,shd->hts/dot_general | solution.py:57
  86.5 9.9 %fusion.13 = f32[8,128,1024]{2,1,0:T(8,128)} fusion(bf16[8,512,1024]{2,1,0:T(8,128)(2,1)} %select_convert_fusion.1, bf16[1024,8,128]{2,0,1:T(8,128)(2,1)S(1)} %fusion), kind=kOutput, calls=%fused_computation.36 | convolution fusion | flops 1073741824 | bytes 13631488 | tf_op jit(solution)/shard_map/hts,the->she/dot_general | solution.py:80
  96.4 4.8 %fusion.22 = f32[8,1024,128]{2,1,0:T(8,128)} fusion(bf16[8,512,1024]{2,1,0:T(8,128)(2,1)S(1)} %select_convert_fusion, bf16[1024,8,128]{2,0,1:T(8,128)(2,1)S(1)} %copy-done.2), kind=kOutput, calls=%fused_computation.45 | convolution fusion | flops 1073741824 | bytes 13631488 | tf_op jit(solution)/shard_map/hts,thd->shd/dot_general | solution.py:77
  101.2 2.9 %multiply_reduce_fusion.1 = bf16[8,128,128]{2,1,0:T(8,128)(2,1)S(1)} fusion(f32[8,8,128,128]{3,2,1,0:T(8,128)} %bitcast.81, f32[8]{0:T(128)S(1)} %compare_convert_fusion.1), kind=kLoop, calls=%fused_computation.13 | loop fusion | flops 1966080 | bytes 4456480 | tf_op jit(solution)/shard_map/reduce_sum | solution.py:30
  108.7 6.4 %fusion.6 = bf16[512,8,128]{0,2,1:T(8,128)(2,1)S(1)} fusion(f32[8,128,512]{2,1,0:T(8,128)S(1)} %fusion.25, bf16[8,512,1024]{2,1,0:T(8,128)(2,1)} %select_convert_fusion.1, f32[512]{0:T(512)S(1)} %get-tuple-element.81, bf16[1024,8,128]{2,1,0:T(8,128)(2,1)S(1)} %copy-done.15), kind=kOutput, calls=%fused_computation.22 | convolution fusion | flops 1075314688 | bytes 13633536 | tf_op jit(solution)/shard_map/hts,shd->thd/dot_general | solution.py:63
  116.6 4.1 %copy.85 = bf16[1024,8,128]{2,1,0:T(8,128)(2,1)} copy(bf16[1024,8,128]{0,2,1:T(8,128)(2,1)} %pad_maximum_fusion) | data formatting | bytes 4194304 | tf_op jit(solution)/shard_map/concatenate | solution.py:88
  120.8 4.7 %all-to-all-start = ((bf16[1024,8,128]{2,1,0:T(8,128)(2,1)}), bf16[1024,8,128]{2,1,0:T(8,128)(2,1)}, u32[]{:S(2)}, u32[]{:S(2)}) async-start(bf16[1024,8,128]{2,1,0:T(8,128)(2,1)} %copy.85), calls=%async_computation | async-start | bytes 4194304 | tf_op jit(solution)/shard_map/all_to_all | solution.py:89
  131.6 6.3 %fusion.3 = bf16[512,8,128]{0,2,1:T(8,128)(2,1)S(1)} fusion(f32[8,128,512]{2,1,0:T(8,128)S(1)} %copy-done.23, bf16[8,512,1024]{2,1,0:T(8,128)(2,1)} %copy-done.12, bf16[1024,8,128]{2,1,0:T(8,128)(2,1)S(1)} %copy-done.18), kind=kOutput, calls=%fused_computation.17 | convolution fusion | flops 1074790400 | bytes 13631488 | tf_op jit(solution)/shard_map/hts,shd->thd/dot_general | solution.py:72
  139.5 4.3 %copy.104 = bf16[1024,8,128]{2,1,0:T(8,128)(2,1)} copy(bf16[1024,8,128]{0,2,1:T(8,128)(2,1)} %pad_maximum_fusion.1) | data formatting | bytes 4194304
  143.8 2.8 %multiply_reduce_fusion = bf16[8,128,128]{2,1,0:T(8,128)(2,1)S(1)} fusion(f32[8,8,128,128]{3,2,1,0:T(8,128)} %bitcast.82, f32[8]{0:T(128)S(1)} %compare_convert_fusion), kind=kLoop, calls=%fused_computation.12 | loop fusion | flops 1966080 | bytes 4456480 | tf_op jit(solution)/shard_map/reduce_sum | solution.py:31
  147.3 2.6 %fusion.2 = bf16[1024,8,128]{2,0,1:T(8,128)(2,1)S(1)} fusion(f32[8,1024,128]{2,1,0:T(8,128)S(1)} %copy-done.8, f32[512,8,128]{2,0,1:T(8,128)S(1)} %copy-done.11, bf16[8,128,128]{2,1,0:T(8,128)(2,1)S(1)} %multiply_reduce_fusion, bf16[1024,8,128]{2,1,0:T(8,128)(2,1)} %param.18), kind=kOutput, calls=%fused_computation.10 | convolution fusion | flops 271581184 | bytes 10747904 | tf_op jit(solution)/shard_map/shj,hij->shi/dot_general | solution.py:82
  149.9 2.7 %copy.105 = bf16[1024,8,128]{2,1,0:T(8,128)(2,1)} copy(bf16[1024,8,128]{2,0,1:T(8,128)(2,1)S(1)} %fusion.2) | data formatting | bytes 4194304
  153.6 2.9 %copy.106 = bf16[1024,8,128]{2,1,0:T(8,128)(2,1)} copy(bf16[1024,8,128]{0,2,1:T(8,128)(2,1)S(1)} %fusion.1) | data formatting | bytes 4194304
  156.5 16.4 %all-to-all-done = bf16[1024,8,128]{2,1,0:T(8,128)(2,1)} async-done(((bf16[1024,8,128]{2,1,0:T(8,128)(2,1)}), bf16[1024,8,128]{2,1,0:T(8,128)(2,1)}, u32[]{:S(2)}, u32[]{:S(2)}) %all-to-all-start) | async-done | bytes 2097184 | tf_op jit(solution)/shard_map/all_to_all | solution.py:89
  172.9 3.3 %copy.139 = bf16[256,4,8,128]{3,2,1,0:T(8,128)(2,1)} copy(bf16[256,4,8,128]{3,2,0,1:T(8,128)(2,1)} %bitcast.6) | data formatting | bytes 4194304 | tf_op jit(solution)/shard_map/all_to_all | solution.py:89
  (77 shorter events, 29.4 us)
Async XLA Ops:
  7.2 4.5 %copy-start.22 = (bf16[256,32,128]{2,1,0:T(8,128)(2,1)S(1)}, bf16[256,32,128]{2,1,0:T(8,128)(2,1)}, u32[]{:S(2)}) copy-start(bf16[256,32,128]{2,1,0:T(8,128)(2,1)} %param.19) | copy-start | bytes 6291460
  7.2 94.0 %all-gather.5.cloned.1.call-start = ((), (), s32[]{:S(2)}) async-start(), calls=%async_computation.2 | async-start | bytes 4718592 | tf_op jit(solution)/shard_map/all_gather | solution.py:22
  13.8 6.5 %copy-start.16 = (bf16[1024,8,128]{2,1,0:T(8,128)(2,1)S(1)}, bf16[1024,8,128]{2,1,0:T(8,128)(2,1)}, u32[]{:S(2)}) copy-start(bf16[1024,8,128]{2,1,0:T(8,128)(2,1)} %param.17) | copy-start | bytes 6291460
  13.8 54.8 %all-to-all-start.1 = ((bf16[256,32,128]{2,0,1:T(8,128)(2,1)}), bf16[256,32,128]{2,0,1:T(8,128)(2,1)}, u32[]{:S(2)}, u32[]{:S(2)}) async-start(bf16[256,32,128]{2,0,1:T(8,128)(2,1)} %copy.87), calls=%async_computation.1 | async-start | bytes 4194304 | tf_op jit(solution)/shard_map/all_to_all | solution.py:9
  20.3 123.5 %all-gather.7.cloned.1.call-start = ((), (), s32[]{:S(2)}) async-start(), calls=%async_computation.3 | async-start | bytes 4718592 | tf_op jit(solution)/shard_map/all_gather | solution.py:23
  20.3 2.5 %copy-start.13 = (bf16[1024,8,128]{2,1,0:T(8,128)(2,1)S(1)}, bf16[1024,8,128]{2,1,0:T(8,128)(2,1)}, u32[]{:S(2)}) copy-start(bf16[1024,8,128]{2,1,0:T(8,128)(2,1)} %param.18) | copy-start | bytes 6291460
  26.3 5.3 %copy-start.1 = (bf16[1024,8,128]{2,0,1:T(8,128)(2,1)}, bf16[1024,8,128]{2,0,1:T(8,128)(2,1)S(1)}, u32[]{:S(2)}) copy-start(bf16[1024,8,128]{2,0,1:T(8,128)(2,1)S(1)} %copy.75) | copy-start | bytes 6291460
  26.8 4.7 %copy-start.17 = (bf16[1024,8,128]{2,1,0:T(8,128)(2,1)S(1)}, bf16[1024,8,128]{2,1,0:T(8,128)(2,1)}, u32[]{:S(2)}) copy-start(bf16[1024,8,128]{2,1,0:T(8,128)(2,1)} %param.17) | copy-start | bytes 6291460
  74.3 2.7 %copy-start.2 = (bf16[1024,8,128]{2,0,1:T(8,128)(2,1)S(1)}, bf16[1024,8,128]{2,0,1:T(8,128)(2,1)}, u32[]{:S(2)}) copy-start(bf16[1024,8,128]{2,0,1:T(8,128)(2,1)} %copy-done.1) | copy-start | bytes 6291460
  77.0 3.2 %copy-start.6 = (bf16[8,512,512]{2,1,0:T(8,128)(2,1)}, bf16[8,512,512]{2,1,0:T(8,128)(2,1)S(1)}, u32[]{:S(2)}) copy-start(bf16[8,512,512]{2,1,0:T(8,128)(2,1)S(1)} %select_convert_fusion.2) | copy-start | bytes 12582916
  77.0 4.5 %copy-start.4 = (bf16[8,512,512]{2,1,0:T(8,128)(2,1)S(1)}, bf16[8,512,512]{2,1,0:T(8,128)(2,1)}, u32[]{:S(2)}) copy-start(bf16[8,512,512]{2,1,0:T(8,128)(2,1)} %select_convert_fusion.3) | copy-start | bytes 12582916
  81.5 2.2 %copy-start.14 = (bf16[1024,8,128]{2,1,0:T(8,128)(2,1)S(1)}, bf16[1024,8,128]{2,1,0:T(8,128)(2,1)}, u32[]{:S(2)}) copy-start(bf16[1024,8,128]{2,1,0:T(8,128)(2,1)} %param.18) | copy-start | bytes 6291460
  86.5 9.9 %copy-start.12 = (bf16[8,512,1024]{2,1,0:T(8,128)(2,1)}, bf16[8,512,1024]{2,1,0:T(8,128)(2,1)S(1)}, u32[]{:S(2)}) copy-start(bf16[8,512,1024]{2,1,0:T(8,128)(2,1)S(1)} %select_convert_fusion) | copy-start | bytes 25165828
  101.2 2.9 %copy-start.3 = (bf16[1024,8,128]{2,0,1:T(8,128)(2,1)S(1)}, bf16[1024,8,128]{2,0,1:T(8,128)(2,1)}, u32[]{:S(2)}) copy-start(bf16[1024,8,128]{2,0,1:T(8,128)(2,1)} %copy-done.1) | copy-start | bytes 6291460
  104.1 2.2 %copy-start.5 = (bf16[8,512,512]{2,1,0:T(8,128)(2,1)S(1)}, bf16[8,512,512]{2,1,0:T(8,128)(2,1)}, u32[]{:S(2)}) copy-start(bf16[8,512,512]{2,1,0:T(8,128)(2,1)} %select_convert_fusion.3) | copy-start | bytes 12582916
  104.6 2.5 %copy-start.20 = (bf16[1024,8,128]{2,0,1:T(8,128)(2,1)S(1)}, bf16[1024,8,128]{2,0,1:T(8,128)(2,1)}, u32[]{:S(2)}) copy-start(bf16[1024,8,128]{2,0,1:T(8,128)(2,1)} %copy.74) | copy-start | bytes 6291460
  120.8 52.1 %all-to-all-start = ((bf16[1024,8,128]{2,1,0:T(8,128)(2,1)}), bf16[1024,8,128]{2,1,0:T(8,128)(2,1)}, u32[]{:S(2)}, u32[]{:S(2)}) async-start(bf16[1024,8,128]{2,1,0:T(8,128)(2,1)} %copy.85), calls=%async_computation | async-start | bytes 4194304 | tf_op jit(solution)/shard_map/all_to_all | solution.py:89
  125.5 2.9 %copy-start.7 = (bf16[8,512,512]{2,1,0:T(8,128)(2,1)S(1)}, bf16[8,512,512]{2,1,0:T(8,128)(2,1)}, u32[]{:S(2)}) copy-start(bf16[8,512,512]{2,1,0:T(8,128)(2,1)} %copy-done.6) | copy-start | bytes 12582916
  129.4 2.2 %copy-start.23 = (f32[8,128,512]{2,1,0:T(8,128)S(1)}, f32[8,128,512]{2,1,0:T(8,128)}, u32[]{:S(2)}) copy-start(f32[8,128,512]{2,1,0:T(8,128)} %fusion.16) | copy-start | bytes 6291460
  139.5 7.1 %copy-start.11 = (f32[512,8,128]{2,0,1:T(8,128)S(1)}, f32[512,8,128]{2,0,1:T(8,128)}, u32[]{:S(2)}) copy-start(f32[512,8,128]{2,0,1:T(8,128)} %convolution_bitcast_fusion.1) | copy-start | bytes 6291460
  143.8 3.4 %copy-start.8 = (f32[8,1024,128]{2,1,0:T(8,128)S(1)}, f32[8,1024,128]{2,1,0:T(8,128)}, u32[]{:S(2)}) copy-start(f32[8,1024,128]{2,1,0:T(8,128)} %fusion.22) | copy-start | bytes 12582916
  147.3 5.3 %copy-start.10 = (f32[512,8,128]{0,2,1:T(8,128)S(1)}, f32[512,8,128]{0,2,1:T(8,128)}, u32[]{:S(2)}) copy-start(f32[512,8,128]{0,2,1:T(8,128)} %convolution_bitcast_fusion) | copy-start | bytes 6291460
  147.3 5.3 %copy-start.19 = (bf16[1024,8,128]{2,1,0:T(8,128)(2,1)S(1)}, bf16[1024,8,128]{2,1,0:T(8,128)(2,1)}, u32[]{:S(2)}) copy-start(bf16[1024,8,128]{2,1,0:T(8,128)(2,1)} %param.17) | copy-start | bytes 6291460
  149.9 2.7 %copy-start = (f32[8,128,1024]{2,1,0:T(8,128)S(1)}, f32[8,128,1024]{2,1,0:T(8,128)}, u32[]{:S(2)}) copy-start(f32[8,128,1024]{2,1,0:T(8,128)} %fusion.13) | copy-start | bytes 12582916
  (4 other events, 6.9 us)
Sparse Core Ops, SparseCore 0:
  11.8 39.2 all-gather.4
  74.4 35.7 all-gather.6
where the time goes:
time: 184 us; the launch traced here: 183 us
  matrix products  63.9 us (35%)
  waiting for transfers between devices  47.5 us (26%)
  local copies, waits for them, and re-layouts  36.4 us (20%)
  between operations  14.3 us (8%)
  starting transfers between devices  11.2 us (6%)
  other arithmetic  9.73 us (5%)
    all_to_all x1, waiting for transfers between devices, per_device(): lax.all_to_all(out_grad, 'head', split_axis=1, concat_axis=0, tiled=True)  31.1 us
    unnamed x55, local copies, waits for them, and re-layouts  25.9 us
    all_to_all x1, waiting for transfers between devices, per_device(): lax.all_to_all(attended_heads, 'head', split_axis=0, concat_axis=1, tiled...  16.4 us
    dot_general x2, matrix products, per_device(): jnp.einsum('hts,the->she', within, grad_block, preferred_element_type=jnp...  12.1 us
    dot_general x2, matrix products, per_device(): jnp.einsum('thd,shd->hts', query_block, key_past, preferred_element_type=...  10.7 us
    dot_general x2, matrix products, per_device(): jnp.einsum('hts,shd->thd', within, value_past, preferred_element_type=jnp...  7.92 us
    dot_general x2, matrix products, per_device(): jnp.einsum('hts,shd->thd', grad_scores, key_past, preferred_element_type=...  7.88 us
    dot_general x2, matrix products, per_device(): jnp.einsum('hts,thd->shd', grad_scores, query_block, preferred_element_ty...  7.63 us
  transfers between devices with their start and end apart: 4, of which 2 were waited for; matrix products, arithmetic and copies ran while one was open for 51% of the time, Pallas kernels for 0%

commit v1 on v0

v1 whole, which is shorter than its diff:
```python
import jax
import jax.numpy as jnp
from jax import lax
from jax.experimental import pallas as pl
from jax.experimental.pallas import tpu as pltpu
from jax.sharding import PartitionSpec as P


F32 = jnp.float32
BF16 = jnp.bfloat16


def dot(lhs, rhs, lhs_dim, rhs_dim):
    return lax.dot_general(
        lhs, rhs, (((lhs_dim,), (rhs_dim,)), ((), ())), preferred_element_type=F32
    )


def iota(rows, dim):
    return lax.broadcasted_iota(jnp.int32, (rows, rows), dim)


def masked(mask, scores):
    return jnp.where(mask, scores, 0.0).astype(BF16)


def key_state_kernel(key_ref, value_ref, key_out, value_out, before_ref, total_ref, running):
    @pl.when(pl.program_id(0) == 0)
    def _():
        running[...] = jnp.zeros_like(running)

    key_out[...] = jnp.swapaxes(key_ref[...], 0, 1)
    value_out[...] = jnp.swapaxes(value_ref[...], 0, 1)
    before_ref[:, 0] = running[...]
    for h in range(running.shape[0]):
        running[h] += dot(key_out[h], value_out[h], 0, 0)
    total_ref[...] = running[...]


def attended_kernel(index_ref, query_ref, key_ref, value_ref, before_ref, prefix_ref, scale_ref, out_ref, held):
    block, rows = query_ref.shape[:2]
    mask = iota(rows, 1) <= iota(rows, 0)
    scale = scale_ref[...]
    first = pl.program_id(0) * block
    for h in range(block):
        query = query_ref[h]
        state = (prefix_ref[h] + before_ref[h, 0]).astype(BF16)
        within = masked(mask, dot(query, key_ref[h], 1, 1))
        total = dot(query, state, 1, 0) + dot(within, value_ref[h], 1, 0)
        held[first + h] = (scale * total).astype(BF16)

    @pl.when(pl.program_id(0) == pl.num_programs(0) - 1)
    def _():
        out_ref[...] = jnp.swapaxes(held[...], 0, 1)


def grad_state_kernel(index_ref, piece_ref, query_ref, scale_ref, grad_ref, state_ref):
    scale = scale_ref[...][:, None, :]
    scaled = (scale * piece_ref[...].astype(F32)).astype(BF16)
    grad_ref[...] = jnp.swapaxes(scaled, 0, 1)
    for h in range(grad_ref.shape[0]):
        state_ref[h] = dot(query_ref[h], grad_ref[h], 0, 0)


def local_grad_kernel(index_ref, query_ref, key_ref, value_ref, grad_ref, before_ref, prefix_ref, *refs):
    query_out, key_out, value_out, held = refs[-4:]
    block, rows = query_ref.shape[:2]
    lower = iota(rows, 1) <= iota(rows, 0)
    upper = iota(rows, 0) <= iota(rows, 1)
    first = pl.program_id(0) * block
    for h in range(block):
        query, key, value, grad = query_ref[h], key_ref[h], value_ref[h], grad_ref[h]
        state = (prefix_ref[h] + before_ref[h, 0]).astype(BF16)
        scores = masked(lower, dot(grad, value, 1, 1))
        held[first + h] = (dot(grad, state, 1, 1) + dot(scores, key, 1, 0)).astype(BF16)
        key_out[h] = dot(masked(upper, dot(value, grad, 1, 1)), query, 1, 0)
        value_out[h] = dot(masked(upper, dot(key, query, 1, 1)), grad, 1, 0)

    @pl.when(pl.program_id(0) == pl.num_programs(0) - 1)
    def _():
        query_out[...] = jnp.swapaxes(held[...], 0, 1)


def later_grad_kernel(index_ref, key_ref, value_ref, key_part, value_part, suffix_ref, *refs):
    states = refs[:-4]
    key_out, value_out, key_held, value_held = refs[-4:]
    c = pl.program_id(0)
    for h in range(key_ref.shape[0]):
        state = suffix_ref[h]
        for r, state_ref in enumerate(states):
            state = state + jnp.where(index_ref[r] > c, state_ref[h], 0.0)
        state = state.astype(BF16)
        key_held[h] = (key_part[h] + dot(value_ref[h], state, 1, 1)).astype(BF16)
        value_held[h] = (value_part[h] + dot(key_ref[h], state, 1, 0)).astype(BF16)
    key_out[...] = jnp.swapaxes(key_held[...], 0, 1)
    value_out[...] = jnp.swapaxes(value_held[...], 0, 1)


def cost(flops, size):
    return pl.CostEstimate(flops=int(flops), bytes_accessed=int(size), transcendentals=0)


def other_segments(total, later, n_seq):
    core = lax.axis_index("seq") % 2
    half = total.shape[0] // 2
    swap = [(i, i ^ 1) for i in range(n_seq)]
    twin = lax.ppermute(total, "seq", swap)
    mine = lax.dynamic_slice_in_dim(total + twin, core * half, half, 0)
    acc = jnp.zeros_like(mine)
    for step in range(n_seq // 2 - 1, 0, -1):
        hops = [(i, i + 2 * step) for i in range(n_seq - 2 * step)]
        if later:
            hops = [(b, a) for a, b in hops]
        acc = acc + lax.ppermute(mine, "seq", hops)
    theirs = lax.ppermute(acc, "seq", swap)
    low = core == 0
    both = jnp.concatenate([jnp.where(low, acc, theirs), jnp.where(low, theirs, acc)], axis=0)
    use_twin = low if later else jnp.logical_not(low)
    return both + jnp.where(use_twin, twin, 0.0)


def per_device(n_seq, n_head, queries, key_vectors, value_vectors, out_grad):
    tok_rows, heads, size = queries.shape
    chunk = out_grad.shape[0]
    n_chunk = tok_rows // chunk
    block = max(heads // 2, 1)
    me = lax.axis_index("head")
    order = sorted(range(1, n_head), reverse=True)
    array = jax.ShapeDtypeStruct
    index = {r: jnp.reshape(me ^ r, (1,)).astype(jnp.int32) for r in range(n_head)}
    chunk_of = jnp.stack([me ^ r for r in range(n_head)]).astype(jnp.int32)

    pieces = {}
    for r in order:
        piece = lax.dynamic_slice_in_dim(out_grad, (me ^ r) * heads, heads, 1)
        pieces[r] = lax.ppermute(piece, "head", [(i, i ^ r) for i in range(n_head)])
    pieces[0] = lax.dynamic_slice_in_dim(out_grad, me * heads, heads, 1)

    position = (lax.axis_index("seq") * tok_rows + lax.iota(jnp.int32, tok_rows)).astype(F32)
    scaling = 1.0 / jnp.sqrt(size * (position + 1.0))
    scale = jnp.broadcast_to(scaling[:, None], (tok_rows, size))

    full_bytes = heads * tok_rows * size * 2
    unit = 2 * heads * tok_rows * size * chunk

    by_token = pl.BlockSpec((chunk, heads, size), lambda c, *_: (c, 0, 0))
    by_head = pl.BlockSpec((heads, chunk, size), lambda c, *_: (0, c, 0))
    all_states = pl.BlockSpec((heads, size, size), lambda *_: (0, 0, 0))
    head_shape = array((heads, tok_rows, size), BF16)
    state_shape = array((heads, size, size), F32)
    key, value, before, key_total = pl.pallas_call(
        key_state_kernel,
        grid=(n_chunk,),
        in_specs=[by_token, by_token],
        out_specs=[
            by_head,
            by_head,
            pl.BlockSpec((heads, 1, size, size), lambda c: (0, c, 0, 0)),
            all_states,
        ],
        out_shape=[head_shape, head_shape, array((heads, n_chunk, size, size), F32), state_shape],
        scratch_shapes=[pltpu.VMEM((heads, size, size), F32)],
        cost_estimate=cost(unit, 5 * full_bytes),
        name="key_state",
    )(key_vectors, value_vectors)
    query = jnp.transpose(queries, (1, 0, 2))
    prefix = other_segments(key_total, False, n_seq)

    rows_spec = pl.BlockSpec((block, chunk, size), lambda h, i: (h, i[0], 0))
    before_spec = pl.BlockSpec((block, 1, size, size), lambda h, i: (h, i[0], 0, 0))
    some_states = pl.BlockSpec((block, size, size), lambda h, i: (h, 0, 0))
    scale_spec = pl.BlockSpec((chunk, size), lambda h, i: (i[0], 0))
    piece_spec = pl.BlockSpec((chunk, heads, size), lambda h, i: (0, 0, 0))

    arrived = {}
    for r in order + [0]:
        part = pl.pallas_call(
            attended_kernel,
            grid_spec=pltpu.PrefetchScalarGridSpec(
                num_scalar_prefetch=1,
                grid=(heads // block,),
                in_specs=[rows_spec] * 3 + [before_spec, some_states, scale_spec],
                out_specs=piece_spec,
                scratch_shapes=[pltpu.VMEM((heads, chunk, size), BF16)],
            ),
            out_shape=array((chunk, heads, size), BF16),
            cost_estimate=cost(3 * unit // n_chunk, 5 * full_bytes // n_chunk),
            name="attended",
        )(index[r], query, key, value, before, prefix, scale)
        arrived[r] = lax.ppermute(part, "head", [(i, i ^ r) for i in range(n_head)]) if r else part

    grads, states = {}, {}
    for r in [0] + order[::-1]:
        grads[r], states[r] = pl.pallas_call(
            grad_state_kernel,
            grid_spec=pltpu.PrefetchScalarGridSpec(
                num_scalar_prefetch=1,
                grid=(1,),
                in_specs=[
                    piece_spec,
                    pl.BlockSpec((heads, chunk, size), lambda h, i: (0, i[0], 0)),
                    scale_spec,
                ],
                out_specs=[pl.BlockSpec((heads, chunk, size), lambda h, i: (0, 0, 0)), all_states],
            ),
            out_shape=[array((heads, chunk, size), BF16), state_shape],
            cost_estimate=cost(unit // n_chunk, 4 * full_bytes // n_chunk),
            name="grad_state",
        )(index[r], pieces[r], query, scale)
    grad_total = sum(states[r] for r in range(1, n_head)) + states[0]
    suffix = other_segments(grad_total, True, n_seq)

    outs = ()
    out_shapes = [
        array((tok_rows, heads, size), BF16),
        array((heads, tok_rows, size), F32),
        array((heads, tok_rows, size), F32),
    ]
    for r in [0] + order[::-1]:
        outs = pl.pallas_call(
            local_grad_kernel,
            grid_spec=pltpu.PrefetchScalarGridSpec(
                num_scalar_prefetch=1,
                grid=(heads // block,),
                in_specs=[rows_spec] * 3
                + [pl.BlockSpec((block, chunk, size), lambda h, i: (h, 0, 0)), before_spec, some_states]
                + [pl.BlockSpec(memory_space=pl.ANY)] * len(outs),
                out_specs=[
                    pl.BlockSpec((chunk, heads, size), lambda h, i: (i[0], 0, 0)),
                    rows_spec,
                    rows_spec,
                ],
                scratch_shapes=[pltpu.VMEM((heads, chunk, size), BF16)],
            ),
            out_shape=out_shapes,
            input_output_aliases={7 + k: k for k in range(len(outs))},
            cost_estimate=cost(7 * unit // n_chunk, 9 * full_bytes // n_chunk),
            name="local_grad",
        )(index[r], query, key, value, grads[r], before, prefix, *outs)
    query_grad, key_part, value_part = outs

    key_grad, value_grad = pl.pallas_call(
        later_grad_kernel,
        grid_spec=pltpu.PrefetchScalarGridSpec(
            num_scalar_prefetch=1,
            grid=(n_chunk,),
            in_specs=[by_head] * 4 + [all_states] * (1 + n_head),
            out_specs=[by_token, by_token],
            scratch_shapes=[pltpu.VMEM((heads, chunk, size), BF16)] * 2,
        ),
        out_shape=[array((tok_rows, heads, size), BF16)] * 2,
        cost_estimate=cost(2 * unit, 8 * full_bytes),
        name="later_grad",
    )(chunk_of, key, value, key_part, value_part, suffix, *[states[r] for r in range(n_head)])

    attended = jnp.zeros((chunk, heads * n_head, size), BF16)
    for r in [0] + order:
        attended = lax.dynamic_update_slice_in_dim(attended, arrived[r], (me ^ r) * heads, 1)
    return attended, query_grad, key_grad, value_grad


def solution(mesh):
    n_seq, n_head = mesh.shape["seq"], mesh.shape["head"]

    def body(*args):
        return per_device(n_seq, n_head, *args)

    return jax.shard_map(
        body,
        mesh=mesh,
        in_specs=(
            P("seq", "head", None),
            P("seq", "head", None),
            P("seq", "head", None),
            P(("seq", "head"), None, None),
        ),
        out_specs=(
            P(("seq", "head"), None, None),
            P("seq", "head", None),
            P("seq", "head", None),
            P("seq", "head", None),
        ),
        check_vma=False,
    )
```

time: 184 us -> 149 us (0.81)
  the two profiles are of different devices: /device:TPU:0 before, /device:TPU:14 now
where the time goes in v1:
time: 149 us; the launch traced here: 148 us
  Pallas kernels  64.3 us (43%)
  waiting for transfers between devices  46.1 us (31%)
  starting transfers between devices  20 us (13%)
  local copies, waits for them, and re-layouts  10.5 us (7%)
  other arithmetic  6.1 us (4%)
    ppermute x3, waiting for transfers between devices, per_device(): pieces[r] = lax.ppermute(piece, 'head', [(i, i ^ r) for i in range(n_head)])  31.5 us
    pallas_call x4, Pallas kernels, per_device(): pl.pallas_call(local_grad_kernel, grid_spec=pltpu.PrefetchScalarGridSpec(...  22.6 us
    pallas_call x4, Pallas kernels, per_device(): pl.pallas_call(attended_kernel, grid_spec=pltpu.PrefetchScalarGridSpec(nu...  15.7 us
    ppermute x3, waiting for transfers between devices, per_device(): lax.ppermute(part, 'head', [(i, i ^ r) for i in range(n_head)])  14.6 us
    ppermute x6, starting transfers between devices, other_segments(): acc = acc + lax.ppermute(mine, 'seq', hops)  11.4 us
    pallas_call x4, Pallas kernels, per_device(): pl.pallas_call(grad_state_kernel, grid_spec=pltpu.PrefetchScalarGridSpec(...  10.4 us
    pallas_call x1, Pallas kernels, per_device(): pl.pallas_call(later_grad_kernel, grid_spec=pltpu.PrefetchScalarGridSpec(...  9.23 us
    pallas_call x1, Pallas kernels, per_device(): pl.pallas_call(key_state_kernel, grid=(n_chunk,), in_specs=[by_token, by_...  6.26 us
  transfers between devices with their start and end apart: 16, of which 4 were waited for; matrix products, arithmetic and copies ran while one was open for 10% of the time, Pallas kernels for 33%

profile of v1, /device:TPU:14, one launch (start us, length us, event | category | flops | bytes accessed | tf_op | source)
XLA Modules:
  0.0 148.0 jit_solution(9686622036350393474)
XLA Ops:
  0.6 6.3 %key_state.1 = (bf16[8,1024,128]{2,1,0:T(8,128)(2,1)}, bf16[8,1024,128]{2,1,0:T(8,128)(2,1)}, f32[8,4,128,128]{3,2,1,0:T(8,128)}, f32[8,128,128]{2,1,0:T(8,128)}) custom-call(bf16[1024,8,128]{2,1,0:T(8,128)(2,1)} %key_ref.1, bf16[1024,8,128]{2,1,0:T(8,128)(2,1)} %value_ref.1), custom_call_target="tpu_custom_call" | custom-call | flops 536870912 | bytes 10485760 | tf_op jit(solution)/shard_map/key_state/pallas_call | solution.py:151
  7.0 3.1 %constant_dynamic-slice_fusion = (bf16[256,8,128]{2,1,0:T(8,128)(2,1)}, bf16[256,8,128]{2,1,0:T(8,128)(2,1)}, bf16[256,8,128]{2,1,0:T(8,128)(2,1)}, bf16[256,8,128]{2,1,0:T(8,128)(2,1)}) fusion(bf16[256,32,128]{2,1,0:T(8,128)(2,1)} %param.7, s32[]{:T(128)S(6)} %select_n.70, s32[]{:T(128)S(6)} %select_n.72, s32[]{:T(128)S(6)} %select_n.71, s32[]{:T(128)S(6)} %select_n.73), kind=kLoop, calls=%fused_computation.13 | loop fusion | bytes 4194320 | tf_op jit(solution)/shard_map/dynamic_slice | solution.py:137
  10.5 2.6 %collective-permute-start.9 = (bf16[256,8,128]{2,1,0:T(8,128)(2,1)}, bf16[256,8,128]{2,1,0:T(8,128)(2,1)}, u32[]{:S(2)}, u32[]{:S(2)}) collective-permute-start(bf16[256,8,128]{2,1,0:T(8,128)(2,1)} %get-tuple-element.57), channel_id=1, source_target_pairs={{0,2},{1,3},{2,0},{3,1},{4,6},{5,7},{6,4},{7,5},{8,10},{9,11},{10,... | collective-permute-start | bytes 1572872 | tf_op jit(solution)/shard_map/ppermute | solution.py:136
  16.3 2.6 %grad_state.7 = (bf16[8,256,128]{2,1,0:T(8,128)(2,1)}, f32[8,128,128]{2,1,0:T(8,128)}) custom-call(s32[1]{0:T(128)} %bitcast.index_ref, bf16[256,8,128]{2,1,0:T(8,128)(2,1)} %get-tuple-element.56.piece_ref, bf16[8,1024,128]{2,1,0:T(8,128)(2,1)} %bitcast.7, f32[1024,128]{1,0:T(8,128)} %broadcast_in_dim.16.scale_ref), custom_call_target="tpu_custom_call" | custom-call | flops 134217728 | bytes 2097152 | tf_op jit(solution)/shard_map/grad_state/pallas_call | solution.py:194
  21.5 11.9 %collective-permute-done.10.piece_ref = bf16[256,8,128]{2,1,0:T(8,128)(2,1)} collective-permute-done((bf16[256,8,128]{2,1,0:T(8,128)(2,1)}, bf16[256,8,128]{2,1,0:T(8,128)(2,1)}, u32[]{:S(2)}, u32[]{:S(2)}) %collective-permute-start.10) | collective-permute-done | bytes 524320 | tf_op jit(solution)/shard_map/ppermute | solution.py:136
  34.7 2.6 %grad_state.6 = (bf16[8,256,128]{2,1,0:T(8,128)(2,1)}, f32[8,128,128]{2,1,0:T(8,128)}) custom-call(s32[1]{0:T(128)} %bitcast.4.index_ref, bf16[256,8,128]{2,1,0:T(8,128)(2,1)} %collective-permute-done.10.piece_ref, bf16[8,1024,128]{2,1,0:T(8,128)(2,1)} %bitcast.8, f32[1024,128]{1,0:T(8,128)} %broadcast_in_dim.16.scale_ref), custom_call_target="tpu_custom_call" | custom-call | flops 134217728 | bytes 2097152 | tf_op jit(solution)/shard_map/grad_state/pallas_call | solution.py:194
  37.3 10.9 %collective-permute-done.9.piece_ref = bf16[256,8,128]{2,1,0:T(8,128)(2,1)} collective-permute-done((bf16[256,8,128]{2,1,0:T(8,128)(2,1)}, bf16[256,8,128]{2,1,0:T(8,128)(2,1)}, u32[]{:S(2)}, u32[]{:S(2)}) %collective-permute-start.9) | collective-permute-done | bytes 524320 | tf_op jit(solution)/shard_map/ppermute | solution.py:136
  48.3 2.6 %grad_state.5 = (bf16[8,256,128]{2,1,0:T(8,128)(2,1)}, f32[8,128,128]{2,1,0:T(8,128)}) custom-call(s32[1]{0:T(128)} %bitcast.3.index_ref, bf16[256,8,128]{2,1,0:T(8,128)(2,1)} %collective-permute-done.9.piece_ref, bf16[8,1024,128]{2,1,0:T(8,128)(2,1)} %bitcast.9, f32[1024,128]{1,0:T(8,128)} %broadcast_in_dim.16.scale_ref), custom_call_target="tpu_custom_call" | custom-call | flops 134217728 | bytes 2097152 | tf_op jit(solution)/shard_map/grad_state/pallas_call | solution.py:194
  50.9 8.6 %collective-permute-done.8.piece_ref = bf16[256,8,128]{2,1,0:T(8,128)(2,1)S(1)} collective-permute-done((bf16[256,8,128]{2,1,0:T(8,128)(2,1)}, bf16[256,8,128]{2,1,0:T(8,128)(2,1)S(1)}, u32[]{:S(2)}, u32[]{:S(2)}) %collective-permute-start.8) | collective-permute-done | bytes 524320 | tf_op jit(solution)/shard_map/ppermute | solution.py:136
  60.3 2.6 %grad_state.4 = (bf16[8,256,128]{2,1,0:T(8,128)(2,1)}, f32[8,128,128]{2,1,0:T(8,128)}) custom-call(s32[1]{0:T(128)} %bitcast.2.index_ref, bf16[256,8,128]{2,1,0:T(8,128)(2,1)} %copy-done.6, bf16[8,1024,128]{2,1,0:T(8,128)(2,1)} %bitcast.10, f32[1024,128]{1,0:T(8,128)} %broadcast_in_dim.16.scale_ref), custom_call_target="tpu_custom_call" | custom-call | flops 134217728 | bytes 2097152 | tf_op jit(solution)/shard_map/grad_state/pallas_call | solution.py:194
  66.6 3.1 %collective-permute-start.12 = (f32[4,128,128]{2,1,0:T(8,128)S(1)}, f32[4,128,128]{2,1,0:T(8,128)}, u32[]{:S(2)}, u32[]{:S(2)}) collective-permute-start(f32[4,128,128]{2,1,0:T(8,128)S(1)} %dynamic-slice_add_fusion), channel_id=1, source_target_pairs={{24,0},{28,4},{25,1},{29,5},{26,2},{30,6},{27,3},{31,7}} | collective-permute-start | bytes 786440 | tf_op jit(solution)/shard_map/ppermute | solution.py:114
  69.7 2.0 %collective-permute-start.13 = (f32[4,128,128]{2,1,0:T(8,128)S(1)}, f32[4,128,128]{2,1,0:T(8,128)}, u32[]{:S(2)}, u32[]{:S(2)}) collective-permute-start(f32[4,128,128]{2,1,0:T(8,128)S(1)} %dynamic-slice_add_fusion), channel_id=1, source_target_pairs={{16,0},{20,4},{24,8},{28,12},{17,1},{21,5},{25,9},{29,13},{18,2},{... | collective-permute-start | bytes 786440 | tf_op jit(solution)/shard_map/ppermute | solution.py:114
  71.6 2.5 %collective-permute-start.14 = (f32[4,128,128]{2,1,0:T(8,128)S(1)}, f32[4,128,128]{2,1,0:T(8,128)}, u32[]{:S(2)}, u32[]{:S(2)}) collective-permute-start(f32[4,128,128]{2,1,0:T(8,128)S(1)} %dynamic-slice_add_fusion), channel_id=1, source_target_pairs={{8,0},{12,4},{16,8},{20,12},{24,16},{28,20},{9,1},{13,5},{17,9},{2... | collective-permute-start | bytes 786440 | tf_op jit(solution)/shard_map/ppermute | solution.py:114
  75.0 3.9 %attended.6 = bf16[256,8,128]{2,1,0:T(8,128)(2,1)} custom-call(s32[1]{0:T(128)} %bitcast.3.index_ref, bf16[8,1024,128]{2,1,0:T(8,128)(2,1)} %bitcast.11, bf16[8,1024,128]{2,1,0:T(8,128)(2,1)} %get-tuple-element.30.key_ref, bf16[8,1024,128]{2,1,0:T(8,128)(2,1)} %get-tuple-element.31.value_ref, f32[8,4,128,128]{3,2,1,0:T(8,128)} %get-tuple-element.32.before_ref, ...), custom_call_target="tpu_custom_call" | custom-call | flops 402653184 | bytes 2621440 | tf_op jit(solution)/shard_map/attended/pallas_call | solution.py:177
  78.9 3.9 %attended.5 = bf16[256,8,128]{2,1,0:T(8,128)(2,1)} custom-call(s32[1]{0:T(128)} %bitcast.2.index_ref, bf16[8,1024,128]{2,1,0:T(8,128)(2,1)} %bitcast.12, bf16[8,1024,128]{2,1,0:T(8,128)(2,1)} %get-tuple-element.30.key_ref, bf16[8,1024,128]{2,1,0:T(8,128)(2,1)} %get-tuple-element.31.value_ref, f32[8,4,128,128]{3,2,1,0:T(8,128)} %get-tuple-element.32.before_ref, ...), custom_call_target="tpu_custom_call" | custom-call | flops 402653184 | bytes 2621440 | tf_op jit(solution)/shard_map/attended/pallas_call | solution.py:177
  82.9 3.9 %attended.4 = bf16[256,8,128]{2,1,0:T(8,128)(2,1)} custom-call(s32[1]{0:T(128)} %bitcast.index_ref, bf16[8,1024,128]{2,1,0:T(8,128)(2,1)} %bitcast.13, bf16[8,1024,128]{2,1,0:T(8,128)(2,1)} %get-tuple-element.30.key_ref, bf16[8,1024,128]{2,1,0:T(8,128)(2,1)} %get-tuple-element.31.value_ref, f32[8,4,128,128]{3,2,1,0:T(8,128)} %get-tuple-element.32.before_ref, ...), custom_call_target="tpu_custom_call" | custom-call | flops 402653184 | bytes 2621440 | tf_op jit(solution)/shard_map/attended/pallas_call | solution.py:177
  88.9 5.7 %local_grad.4 = (bf16[1024,8,128]{2,1,0:T(8,128)(2,1)}, f32[8,1024,128]{2,1,0:T(8,128)}, f32[8,1024,128]{2,1,0:T(8,128)}) custom-call(s32[1]{0:T(128)} %bitcast.index_ref, bf16[8,1024,128]{2,1,0:T(8,128)(2,1)} %bitcast.14, bf16[8,1024,128]{2,1,0:T(8,128)(2,1)} %get-tuple-element.30.key_ref, bf16[8,1024,128]{2,1,0:T(8,128)(2,1)} %get-tuple-element.31.value_ref, ...), custom_call_target="tpu_custom_call" | custom-call | flops 939524096 | bytes 4718592 | tf_op jit(solution)/shard_map/local_grad/pallas_call | solution.py:220
  94.5 5.7 %local_grad.5 = (bf16[1024,8,128]{2,1,0:T(8,128)(2,1)}, f32[8,1024,128]{2,1,0:T(8,128)}, f32[8,1024,128]{2,1,0:T(8,128)}) custom-call(s32[1]{0:T(128)} %bitcast.4.index_ref, bf16[8,1024,128]{2,1,0:T(8,128)(2,1)} %bitcast.15, bf16[8,1024,128]{2,1,0:T(8,128)(2,1)} %get-tuple-element.30.key_ref, ...), custom_call_target="tpu_custom_call", output_to_operand_aliasing={{0}: (7, {}), {1}: (8, {}), {2}: (9, {})} | custom-call | flops 939524096 | bytes 4718592 | tf_op jit(solution)/shard_map/local_grad/pallas_call | solution.py:220
  100.2 5.7 %local_grad.6 = (bf16[1024,8,128]{2,1,0:T(8,128)(2,1)}, f32[8,1024,128]{2,1,0:T(8,128)}, f32[8,1024,128]{2,1,0:T(8,128)}) custom-call(s32[1]{0:T(128)} %bitcast.3.index_ref, bf16[8,1024,128]{2,1,0:T(8,128)(2,1)} %bitcast.16, bf16[8,1024,128]{2,1,0:T(8,128)(2,1)} %get-tuple-element.30.key_ref, ...), custom_call_target="tpu_custom_call", output_to_operand_aliasing={{0}: (7, {}), {1}: (8, {}), {2}: (9, {})} | custom-call | flops 939524096 | bytes 4718592 | tf_op jit(solution)/shard_map/local_grad/pallas_call | solution.py:220
  105.9 3.9 %attended.7 = bf16[256,8,128]{2,1,0:T(8,128)(2,1)} custom-call(s32[1]{0:T(128)} %bitcast.4.index_ref, bf16[8,1024,128]{2,1,0:T(8,128)(2,1)} %bitcast.17, bf16[8,1024,128]{2,1,0:T(8,128)(2,1)} %get-tuple-element.30.key_ref, bf16[8,1024,128]{2,1,0:T(8,128)(2,1)} %get-tuple-element.31.value_ref, f32[8,4,128,128]{3,2,1,0:T(8,128)} %get-tuple-element.32.before_ref, ...), custom_call_target="tpu_custom_call" | custom-call | flops 402653184 | bytes 2621440 | tf_op jit(solution)/shard_map/attended/pallas_call | solution.py:177
  109.8 2.7 %collective-permute-start.7 = (bf16[256,8,128]{2,1,0:T(8,128)(2,1)}, bf16[256,8,128]{2,1,0:T(8,128)(2,1)}, u32[]{:S(2)}, u32[]{:S(2)}) collective-permute-start(bf16[256,8,128]{2,1,0:T(8,128)(2,1)} %attended.7), channel_id=1, source_target_pairs={{0,1},{1,0},{2,3},{3,2},{4,5},{5,4},{6,7},{7,6},{8,9},{9,8},{10,11... | collective-permute-start | bytes 1572872 | tf_op jit(solution)/shard_map/ppermute | solution.py:190
  112.6 5.6 %local_grad.7 = (bf16[1024,8,128]{2,1,0:T(8,128)(2,1)}, f32[8,1024,128]{2,1,0:T(8,128)}, f32[8,1024,128]{2,1,0:T(8,128)}) custom-call(s32[1]{0:T(128)} %bitcast.2.index_ref, bf16[8,1024,128]{2,1,0:T(8,128)(2,1)} %bitcast.18, bf16[8,1024,128]{2,1,0:T(8,128)(2,1)} %get-tuple-element.30.key_ref, ...), custom_call_target="tpu_custom_call", output_to_operand_aliasing={{0}: (7, {}), {1}: (8, {}), {2}: (9, {})} | custom-call | flops 939524096 | bytes 4718592 | tf_op jit(solution)/shard_map/local_grad/pallas_call | solution.py:220
  119.4 14.6 %collective-permute-done.5 = bf16[256,8,128]{2,1,0:T(8,128)(2,1)} collective-permute-done((bf16[256,8,128]{2,1,0:T(8,128)(2,1)}, bf16[256,8,128]{2,1,0:T(8,128)(2,1)}, u32[]{:S(2)}, u32[]{:S(2)}) %collective-permute-start.5) | collective-permute-done | bytes 524320 | tf_op jit(solution)/shard_map/ppermute | solution.py:190
  138.6 9.2 %later_grad.1 = (bf16[1024,8,128]{2,1,0:T(8,128)(2,1)}, bf16[1024,8,128]{2,1,0:T(8,128)(2,1)}) custom-call(s32[4]{0:T(128)} %pad_add_fusion.index_ref, bf16[8,1024,128]{2,1,0:T(8,128)(2,1)} %get-tuple-element.30.key_ref, bf16[8,1024,128]{2,1,0:T(8,128)(2,1)} %get-tuple-element.31.value_ref, f32[8,1024,128]{2,1,0:T(8,128)} %get-tuple-element.48.key_part, ...), custom_call_target="tpu_custom_call" | custom-call | flops 1073741824 | bytes 16777216 | tf_op jit(solution)/shard_map/later_grad/pallas_call | solution.py:242
  (57 shorter events, 20.7 us)
Async XLA Ops:
  6.9 12.0 %collective-permute-start = (f32[8,128,128]{2,1,0:T(8,128)}, f32[8,128,128]{2,1,0:T(8,128)S(1)}, u32[]{:S(2)}, u32[]{:S(2)}) collective-permute-start(f32[8,128,128]{2,1,0:T(8,128)} %get-tuple-element.33), channel_id=1, source_target_pairs={{0,4},{4,0},{8,12},{12,8},{16,20},{20,16},{24,28},{28,24},{1,5},{5... | collective-permute-start | bytes 1572872 | tf_op jit(solution)/shard_map/ppermute | solution.py:107
  7.0 6.6 %copy-start.5 = (bf16[1024,8,128]{2,1,0:T(8,128)(2,1)S(1)}, bf16[1024,8,128]{2,1,0:T(8,128)(2,1)}, u32[]{:S(2)}) copy-start(bf16[1024,8,128]{2,1,0:T(8,128)(2,1)} %param.4) | copy-start | bytes 6291460
  10.1 23.3 %collective-permute-start.10 = (bf16[256,8,128]{2,1,0:T(8,128)(2,1)}, bf16[256,8,128]{2,1,0:T(8,128)(2,1)}, u32[]{:S(2)}, u32[]{:S(2)}) collective-permute-start(bf16[256,8,128]{2,1,0:T(8,128)(2,1)} %get-tuple-element.59), channel_id=1, source_target_pairs={{0,1},{1,0},{2,3},{3,2},{4,5},{5,4},{6,7},{7,6},{8,9},{9,8},{10,11... | collective-permute-start | bytes 1572872 | tf_op jit(solution)/shard_map/ppermute | solution.py:136
  10.5 37.7 %collective-permute-start.9 = (bf16[256,8,128]{2,1,0:T(8,128)(2,1)}, bf16[256,8,128]{2,1,0:T(8,128)(2,1)}, u32[]{:S(2)}, u32[]{:S(2)}) collective-permute-start(bf16[256,8,128]{2,1,0:T(8,128)(2,1)} %get-tuple-element.57), channel_id=1, source_target_pairs={{0,2},{1,3},{2,0},{3,1},{4,6},{5,7},{6,4},{7,5},{8,10},{9,11},{10,... | collective-permute-start | bytes 1572872 | tf_op jit(solution)/shard_map/ppermute | solution.py:136
  13.1 46.4 %collective-permute-start.8 = (bf16[256,8,128]{2,1,0:T(8,128)(2,1)}, bf16[256,8,128]{2,1,0:T(8,128)(2,1)S(1)}, u32[]{:S(2)}, u32[]{:S(2)}) collective-permute-start(bf16[256,8,128]{2,1,0:T(8,128)(2,1)} %get-tuple-element.58), channel_id=1, source_target_pairs={{0,3},{1,2},{2,1},{3,0},{4,7},{5,6},{6,5},{7,4},{8,11},{9,10},{10,... | collective-permute-start | bytes 1572872 | tf_op jit(solution)/shard_map/ppermute | solution.py:136
  15.2 3.7 %copy-start.7 = (f32[8,128,128]{2,1,0:T(8,128)S(1)}, f32[8,128,128]{2,1,0:T(8,128)}, u32[]{:S(2)}) copy-start(f32[8,128,128]{2,1,0:T(8,128)} %get-tuple-element.33) | copy-start | bytes 1572868
  18.9 45.2 %collective-permute-start.1 = (f32[4,128,128]{2,1,0:T(8,128)S(1)}, f32[4,128,128]{2,1,0:T(8,128)}, u32[]{:S(2)}, u32[]{:S(2)}) collective-permute-start(f32[4,128,128]{2,1,0:T(8,128)S(1)} %dynamic-slice_add_fusion.1), channel_id=1, source_target_pairs={{0,24},{4,28},{1,25},{5,29},{2,26},{6,30},{3,27},{7,31}} | collective-permute-start | bytes 786440 | tf_op jit(solution)/shard_map/ppermute | solution.py:114
  20.2 43.9 %collective-permute-start.2 = (f32[4,128,128]{2,1,0:T(8,128)S(1)}, f32[4,128,128]{2,1,0:T(8,128)}, u32[]{:S(2)}, u32[]{:S(2)}) collective-permute-start(f32[4,128,128]{2,1,0:T(8,128)S(1)} %dynamic-slice_add_fusion.1), channel_id=1, source_target_pairs={{0,16},{4,20},{8,24},{12,28},{1,17},{5,21},{9,25},{13,29},{2,18},{... | collective-permute-start | bytes 786440 | tf_op jit(solution)/shard_map/ppermute | solution.py:114
  33.4 30.8 %collective-permute-start.3 = (f32[4,128,128]{2,1,0:T(8,128)S(1)}, f32[4,128,128]{2,1,0:T(8,128)}, u32[]{:S(2)}, u32[]{:S(2)}) collective-permute-start(f32[4,128,128]{2,1,0:T(8,128)S(1)} %dynamic-slice_add_fusion.1), channel_id=1, source_target_pairs={{0,8},{4,12},{8,16},{12,20},{16,24},{20,28},{1,9},{5,13},{9,17},{1... | collective-permute-start | bytes 786440 | tf_op jit(solution)/shard_map/ppermute | solution.py:114
  50.8 12.1 %copy-start = (f32[8,128,128]{2,1,0:T(8,128)S(1)}, f32[8,128,128]{2,1,0:T(8,128)}, u32[]{:S(2)}) copy-start(f32[8,128,128]{2,1,0:T(8,128)} %get-tuple-element.53.refs_0_) | copy-start | bytes 1572868
  50.9 12.1 %copy-start.1 = (f32[8,128,128]{2,1,0:T(8,128)S(1)}, f32[8,128,128]{2,1,0:T(8,128)}, u32[]{:S(2)}) copy-start(f32[8,128,128]{2,1,0:T(8,128)} %get-tuple-element.50.refs_1_) | copy-start | bytes 1572868
  50.9 12.1 %copy-start.2 = (f32[8,128,128]{2,1,0:T(8,128)S(1)}, f32[8,128,128]{2,1,0:T(8,128)}, u32[]{:S(2)}) copy-start(f32[8,128,128]{2,1,0:T(8,128)} %get-tuple-element.51.refs_2_) | copy-start | bytes 1572868
  59.5 0.8 copy-start.6
  64.1 2.5 %collective-permute-start.11 = (f32[8,128,128]{2,1,0:T(8,128)S(1)}, f32[8,128,128]{2,1,0:T(8,128)S(1)}, u32[]{:S(2)}, u32[]{:S(2)}) collective-permute-start(f32[8,128,128]{2,1,0:T(8,128)S(1)} %add_add_fusion), channel_id=1, source_target_pairs={{0,4},{4,0},{8,12},{12,8},{16,20},{20,16},{24,28},{28,24},{1,5},{5... | collective-permute-start | bytes 1572872 | tf_op jit(solution)/shard_map/ppermute | solution.py:107
  65.3 8.8 %collective-permute-start.4 = (f32[4,128,128]{2,1,0:T(8,128)S(1)}, f32[4,128,128]{2,1,0:T(8,128)S(1)}, u32[]{:S(2)}, u32[]{:S(2)}) collective-permute-start(f32[4,128,128]{2,1,0:T(8,128)S(1)} %add_add_fusion.2), channel_id=1, source_target_pairs={{0,4},{4,0},{8,12},{12,8},{16,20},{20,16},{24,28},{28,24},{1,5},{5... | collective-permute-start | bytes 786440 | tf_op jit(solution)/shard_map/ppermute | solution.py:115
  66.6 43.3 %collective-permute-start.12 = (f32[4,128,128]{2,1,0:T(8,128)S(1)}, f32[4,128,128]{2,1,0:T(8,128)}, u32[]{:S(2)}, u32[]{:S(2)}) collective-permute-start(f32[4,128,128]{2,1,0:T(8,128)S(1)} %dynamic-slice_add_fusion), channel_id=1, source_target_pairs={{24,0},{28,4},{25,1},{29,5},{26,2},{30,6},{27,3},{31,7}} | collective-permute-start | bytes 786440 | tf_op jit(solution)/shard_map/ppermute | solution.py:114
  69.7 48.5 %collective-permute-start.13 = (f32[4,128,128]{2,1,0:T(8,128)S(1)}, f32[4,128,128]{2,1,0:T(8,128)}, u32[]{:S(2)}, u32[]{:S(2)}) collective-permute-start(f32[4,128,128]{2,1,0:T(8,128)S(1)} %dynamic-slice_add_fusion), channel_id=1, source_target_pairs={{16,0},{20,4},{24,8},{28,12},{17,1},{21,5},{25,9},{29,13},{18,2},{... | collective-permute-start | bytes 786440 | tf_op jit(solution)/shard_map/ppermute | solution.py:114
  71.6 46.6 %collective-permute-start.14 = (f32[4,128,128]{2,1,0:T(8,128)S(1)}, f32[4,128,128]{2,1,0:T(8,128)}, u32[]{:S(2)}, u32[]{:S(2)}) collective-permute-start(f32[4,128,128]{2,1,0:T(8,128)S(1)} %dynamic-slice_add_fusion), channel_id=1, source_target_pairs={{8,0},{12,4},{16,8},{20,12},{24,16},{28,20},{9,1},{13,5},{17,9},{2... | collective-permute-start | bytes 786440 | tf_op jit(solution)/shard_map/ppermute | solution.py:114
  86.8 1.9 %copy-start.4 = (bf16[256,8,128]{2,1,0:T(8,128)(2,1)S(1)}, bf16[256,8,128]{2,1,0:T(8,128)(2,1)}, u32[]{:S(2)}) copy-start(bf16[256,8,128]{2,1,0:T(8,128)(2,1)} %attended.4) | copy-start | bytes 1572868
  86.8 48.4 %collective-permute-start.6 = (bf16[256,8,128]{2,1,0:T(8,128)(2,1)}, bf16[256,8,128]{2,1,0:T(8,128)(2,1)}, u32[]{:S(2)}, u32[]{:S(2)}) collective-permute-start(bf16[256,8,128]{2,1,0:T(8,128)(2,1)} %attended.6), channel_id=1, source_target_pairs={{0,2},{1,3},{2,0},{3,1},{4,6},{5,7},{6,4},{7,5},{8,10},{9,11},{10,... | collective-permute-start | bytes 1572872 | tf_op jit(solution)/shard_map/ppermute | solution.py:190
  86.8 47.2 %collective-permute-start.5 = (bf16[256,8,128]{2,1,0:T(8,128)(2,1)}, bf16[256,8,128]{2,1,0:T(8,128)(2,1)}, u32[]{:S(2)}, u32[]{:S(2)}) collective-permute-start(bf16[256,8,128]{2,1,0:T(8,128)(2,1)} %attended.5), channel_id=1, source_target_pairs={{0,3},{1,2},{2,1},{3,0},{4,7},{5,6},{6,5},{7,4},{8,11},{9,10},{10,... | collective-permute-start | bytes 1572872 | tf_op jit(solution)/shard_map/ppermute | solution.py:190
  109.8 26.5 %collective-permute-start.7 = (bf16[256,8,128]{2,1,0:T(8,128)(2,1)}, bf16[256,8,128]{2,1,0:T(8,128)(2,1)}, u32[]{:S(2)}, u32[]{:S(2)}) collective-permute-start(bf16[256,8,128]{2,1,0:T(8,128)(2,1)} %attended.7), channel_id=1, source_target_pairs={{0,1},{1,0},{2,3},{3,2},{4,5},{5,4},{6,7},{7,6},{8,9},{9,8},{10,11... | collective-permute-start | bytes 1572872 | tf_op jit(solution)/shard_map/ppermute | solution.py:190
  119.4 18.2 %collective-permute-start.15 = (f32[4,128,128]{2,1,0:T(8,128)S(1)}, f32[4,128,128]{2,1,0:T(8,128)S(1)}, u32[]{:S(2)}, u32[]{:S(2)}) collective-permute-start(f32[4,128,128]{2,1,0:T(8,128)S(1)} %add_add_fusion.1), channel_id=1, source_target_pairs={{0,4},{4,0},{8,12},{12,8},{16,20},{20,16},{24,28},{28,24},{1,5},{5... | collective-permute-start | bytes 786440 | tf_op jit(solution)/shard_map/ppermute | solution.py:115
  137.5 10.3 %copy-start.3 = (bf16[256,32,128]{2,1,0:T(8,128)(2,1)}, bf16[256,32,128]{2,1,0:T(8,128)(2,1)S(1)}, u32[]{:S(2)}) copy-start(bf16[256,32,128]{2,1,0:T(8,128)(2,1)S(1)} %constant_dynamic-update-slice_fusion) | copy-start | bytes 6291460

commit v2 on v1

v2 whole, which is shorter than its diff:
```python
import jax
import jax.numpy as jnp
from jax import lax
from jax.experimental import pallas as pl
from jax.experimental.pallas import tpu as pltpu
from jax.sharding import PartitionSpec as P


F32 = jnp.float32
BF16 = jnp.bfloat16
VMEM_LIMIT = 20 * 1024 * 1024
IN_VMEM = ('place', 'pick', 'local_grad', 'later_grad', 'grad_state', 'grad_state_own', 'attended')


def dot(lhs, rhs, lhs_dim, rhs_dim):
    return lax.dot_general(
        lhs, rhs, (((lhs_dim,), (rhs_dim,)), ((), ())), preferred_element_type=F32
    )


def iota(rows, dim):
    return lax.broadcasted_iota(jnp.int32, (rows, rows), dim)


def masked(mask, scores):
    return jnp.where(mask, scores, 0.0).astype(BF16)


def key_state_kernel(key_ref, value_ref, key_out, value_out, before_ref, total_ref, running):
    @pl.when(pl.program_id(0) == 0)
    def _():
        running[...] = jnp.zeros_like(running)

    key_out[...] = jnp.swapaxes(key_ref[...], 0, 1)
    value_out[...] = jnp.swapaxes(value_ref[...], 0, 1)
    before_ref[:, 0] = running[...]
    for h in range(running.shape[0]):
        running[h] += dot(key_out[h], value_out[h], 0, 0)
    total_ref[...] = running[...]


def base_state(held_refs, core, j, later, half, h):
    twin_ref, mine_ref, theirs_ref = held_refs
    use_twin = core == (0 if later else 1)
    own = jnp.where(core == j, mine_ref[h], theirs_ref[h])
    return own + jnp.where(use_twin, twin_ref[j * half + h], 0.0)


def attended_kernel(n_head, index_ref, query_ref, key_ref, value_ref, before_ref, scale_ref, *refs):
    prefix_refs, outs, held, base = refs[:3], refs[3:-2], refs[-2], refs[-1]
    r, j = pl.program_id(0), pl.program_id(1)
    half, rows = query_ref.shape[:2]
    mask = iota(rows, 1) <= iota(rows, 0)
    scale = scale_ref[...]

    @pl.when(r == 0)
    def _():
        for h in range(half):
            base[j * half + h] = base_state(prefix_refs, index_ref[1], j, False, half, h)

    for h in range(half):
        query = query_ref[h]
        state = (base[j * half + h] + before_ref[h, 0]).astype(BF16)
        within = masked(mask, dot(query, key_ref[h], 1, 1))
        total = dot(query, state, 1, 0) + dot(within, value_ref[h], 1, 0)
        held[j * half + h] = (scale * total).astype(BF16)
    for step in range(n_head):

        @pl.when((j == 1) & (r == step))
        def _():
            outs[step - 1][...] = jnp.swapaxes(held[...], 0, 1)


def grad_state_kernel(n_piece, index_ref, query_ref, scale_ref, *refs):
    pieces = refs[:n_piece]
    grad_ref, state_ref, total_ref = refs[-3:]
    step = pl.program_id(0)
    scale = scale_ref[...][:, None, :]
    for k, piece_ref in enumerate(pieces):

        @pl.when(step == k)
        def _():
            scaled = (scale * piece_ref[...].astype(F32)).astype(BF16)
            grad_ref[...] = jnp.swapaxes(scaled, 0, 1)

    @pl.when(step == 0)
    def _():
        total_ref[...] = refs[n_piece][...] if len(refs) > n_piece + 3 else jnp.zeros_like(total_ref)

    for h in range(grad_ref.shape[0]):
        state = dot(query_ref[h], grad_ref[h], 0, 0)
        state_ref[0, h] = state
        total_ref[h] += state


def local_grad_kernel(index_ref, query_ref, key_ref, value_ref, grad_ref, before_ref, *refs):
    prefix_refs = refs[:3]
    query_out, key_out, value_out, held, base = refs[3:]
    j = pl.program_id(1)
    half, rows = query_ref.shape[:2]
    lower = iota(rows, 1) <= iota(rows, 0)
    upper = iota(rows, 0) <= iota(rows, 1)

    @pl.when(pl.program_id(0) == 0)
    def _():
        for h in range(half):
            base[j * half + h] = base_state(prefix_refs, index_ref[1], j, False, half, h)

    for h in range(half):
        query, key, value, grad = query_ref[h], key_ref[h], value_ref[h], grad_ref[h]
        state = (base[j * half + h] + before_ref[h, 0]).astype(BF16)
        scores = masked(lower, dot(grad, value, 1, 1))
        held[j * half + h] = (dot(grad, state, 1, 1) + dot(scores, key, 1, 0)).astype(BF16)
        key_out[h] = dot(masked(upper, dot(value, grad, 1, 1)), query, 1, 0)
        value_out[h] = dot(masked(upper, dot(key, query, 1, 1)), grad, 1, 0)

    @pl.when(j == 1)
    def _():
        query_out[...] = jnp.swapaxes(held[...], 0, 1)


def later_grad_kernel(index_ref, key_ref, value_ref, key_part, value_part, state_ref, *refs):
    suffix_refs = refs[:3]
    key_out, value_out, running, key_held, value_held = refs[3:]
    half = running.shape[0] // 2

    @pl.when(pl.program_id(0) == 0)
    def _():
        for h in range(2 * half):
            running[h] = base_state(suffix_refs, index_ref[1], h // half, True, half, h % half)

    for h in range(2 * half):
        state = running[h].astype(BF16)
        running[h] += state_ref[0, h]
        key_held[h] = (key_part[h] + dot(value_ref[h], state, 1, 1)).astype(BF16)
        value_held[h] = (value_part[h] + dot(key_ref[h], state, 1, 0)).astype(BF16)
    key_out[...] = jnp.swapaxes(key_held[...], 0, 1)
    value_out[...] = jnp.swapaxes(value_held[...], 0, 1)


def pick_kernel(steps, heads, index_ref, source_ref, *refs):
    outs, sem = refs[:-1], refs[-1]
    copies = []
    for k, step in enumerate(steps):
        at = pl.ds(pl.multiple_of((index_ref[0] ^ step) * heads, heads), heads)
        copies.append(pltpu.make_async_copy(source_ref.at[:, at], outs[k], sem.at[k]))
    for copy in copies:
        copy.start()
    for copy in copies:
        copy.wait()


def place_kernel(steps, heads, index_ref, *refs):
    pieces, out_ref, sem = refs[: len(steps)], refs[-2], refs[-1]
    copies = []
    for k, step in enumerate(steps):
        at = pl.ds(pl.multiple_of((index_ref[0] ^ step) * heads, heads), heads)
        copies.append(pltpu.make_async_copy(pieces[k], out_ref.at[:, at], sem.at[k]))
    for copy in copies:
        copy.start()
    for copy in copies:
        copy.wait()


def cost(flops, size):
    return pl.CostEstimate(flops=int(flops), bytes_accessed=int(size), transcendentals=0)


def other_segments(total, later, n_seq):
    core = lax.axis_index("seq") % 2
    half = total.shape[0] // 2
    swap = [(i, i ^ 1) for i in range(n_seq)]
    twin = lax.ppermute(total, "seq", swap)
    mine = lax.dynamic_slice_in_dim(total + twin, core * half, half, 0)
    acc = jnp.zeros_like(mine)
    for step in range(n_seq // 2 - 1, 0, -1):
        hops = [(i, i + 2 * step) for i in range(n_seq - 2 * step)]
        if later:
            hops = [(b, a) for a, b in hops]
        acc = acc + lax.ppermute(mine, "seq", hops)
    theirs = lax.ppermute(acc, "seq", swap)
    return twin, acc, theirs


def per_device(n_seq, n_head, queries, key_vectors, value_vectors, out_grad):
    tok_rows, heads, size = queries.shape
    chunk = out_grad.shape[0]
    n_chunk = tok_rows // chunk
    me = lax.axis_index("head")
    order = sorted(range(1, n_head), reverse=True)
    array = jax.ShapeDtypeStruct
    core = lax.axis_index("seq") % 2
    place = jnp.stack([me, core]).astype(jnp.int32)
    any_spec = pl.BlockSpec(memory_space=pl.ANY)

    def call(kernel, grid, in_specs, out_specs, out_shape, scratch, estimate, name, aliases={}):
        small = {"vmem_limit_bytes": VMEM_LIMIT} if name in IN_VMEM else {}
        return pl.pallas_call(
            kernel,
            grid_spec=pltpu.PrefetchScalarGridSpec(
                num_scalar_prefetch=1,
                grid=grid,
                in_specs=in_specs,
                out_specs=out_specs,
                scratch_shapes=scratch,
            ),
            out_shape=out_shape,
            input_output_aliases=aliases,
            cost_estimate=estimate,
            compiler_params=pltpu.CompilerParams(**small),
        )

    whole_piece = pl.BlockSpec((chunk, heads, size), lambda *_: (0, 0, 0))
    piece_shape = array((chunk, heads, size), BF16)
    in_vmem = pl.BlockSpec(memory_space=pltpu.VMEM)
    aligned = heads % 8 == 0

    def hbm(*values):
        return [pltpu.with_memory_space_constraint(value, pltpu.HBM) for value in values]

    def pick(steps):
        if not aligned:
            return [lax.dynamic_slice_in_dim(out_grad, (me ^ r) * heads, heads, 1) for r in steps]
        return call(
            lambda *refs: pick_kernel(steps, heads, *refs),
            (1,),
            [any_spec],
            [in_vmem] * len(steps),
            [piece_shape] * len(steps),
            [pltpu.SemaphoreType.DMA((len(steps),))],
            cost(0, 4 * chunk * heads * size * len(steps)),
            "pick",
        )(place, *hbm(out_grad))

    pieces = {}
    picked = dict(zip(order[:1], pick(order[:1])))
    picked.update(zip(order[1:] + [0], pick(order[1:] + [0])))
    for r in order:
        pieces[r] = lax.ppermute(picked[r], "head", [(i, i ^ r) for i in range(n_head)])
    pieces[0] = picked[0]

    position = (lax.axis_index("seq") * tok_rows + lax.iota(jnp.int32, tok_rows)).astype(F32)
    scaling = 1.0 / jnp.sqrt(size * (position + 1.0))
    scale = jnp.broadcast_to(scaling[:, None], (tok_rows, size))

    full_bytes = heads * tok_rows * size * 2
    unit = 2 * heads * tok_rows * size * chunk
    half = heads // 2

    by_token = pl.BlockSpec((chunk, heads, size), lambda c, *_: (c, 0, 0))
    by_head = pl.BlockSpec((heads, chunk, size), lambda c, *_: (0, c, 0))
    all_states = pl.BlockSpec((heads, size, size), lambda *_: (0, 0, 0))
    head_shape = array((heads, tok_rows, size), BF16)
    state_shape = array((heads, size, size), F32)
    states_shape = array((n_chunk, heads, size, size), F32)
    key, value, before, key_total = pl.pallas_call(
        key_state_kernel,
        grid=(n_chunk,),
        in_specs=[by_token, by_token],
        out_specs=[
            by_head,
            by_head,
            pl.BlockSpec((heads, 1, size, size), lambda c: (0, c, 0, 0)),
            all_states,
        ],
        out_shape=[head_shape, head_shape, array((heads, n_chunk, size, size), F32), state_shape],
        scratch_shapes=[pltpu.VMEM((heads, size, size), F32)],
        cost_estimate=cost(unit, 5 * full_bytes),
        name="key_state",
    )(key_vectors, value_vectors)
    query = jnp.transpose(queries, (1, 0, 2))
    prefix = other_segments(key_total, False, n_seq)

    half_states = pl.BlockSpec((half, size, size), lambda *_: (0, 0, 0))
    other_specs = [all_states, half_states, half_states]

    def rows_of(r, j, i):
        return (j, i[0] ^ r, 0)

    rows_spec = pl.BlockSpec((half, chunk, size), rows_of)
    *parts, attended = call(
        lambda *refs: attended_kernel(n_head, *refs),
        (n_head, 2),
        [rows_spec] * 3
        + [
            pl.BlockSpec((half, 1, size, size), lambda r, j, i: (j, i[0] ^ r, 0, 0)),
            pl.BlockSpec((chunk, size), lambda r, j, i: (i[0] ^ r, 0)),
        ]
        + other_specs,
        [whole_piece] * (n_head - 1)
        + ([pl.BlockSpec((chunk, heads, size), lambda r, j, i: (0, i[0], 0))] if aligned else [whole_piece]),
        [piece_shape] * (n_head - 1)
        + ([array((chunk, heads * n_head, size), BF16)] if aligned else [piece_shape]),
        [pltpu.VMEM((heads, chunk, size), BF16), pltpu.VMEM((heads, size, size), F32)],
        cost(3 * unit, 5 * full_bytes),
        "attended",
    )(place, *hbm(query, key, value, before, scale), *prefix)
    arrived = {}
    for r in order:
        arrived[r] = lax.ppermute(parts[r - 1], "head", [(i, i ^ r) for i in range(n_head)])

    def grad_state(name, count, first, extra):
        def at(step, i):
            return i[0] ^ (step + first)

        return call(
            lambda *refs: grad_state_kernel(count, *refs[: 3 + count], *refs[3 + count : -3][:1], *refs[-3:]),
            (count,),
            [
                pl.BlockSpec((heads, chunk, size), lambda s, i: (0, at(s, i), 0)),
                pl.BlockSpec((chunk, size), lambda s, i: (at(s, i), 0)),
            ]
            + [whole_piece] * count
            + ([all_states, any_spec, any_spec] if extra else []),
            [
                pl.BlockSpec((heads, chunk, size), lambda s, i: (0, at(s, i), 0)),
                pl.BlockSpec((1, heads, size, size), lambda s, i: (at(s, i), 0, 0, 0)),
                all_states,
            ],
            [head_shape, states_shape, state_shape],
            [],
            cost(unit * count // n_chunk, 4 * full_bytes * count // n_chunk),
            name,
            {4 + count: 0, 5 + count: 1} if extra else {},
        )(place, *hbm(query, scale), *[pieces[first + k] for k in range(count)], *extra)

    grad, states, total = grad_state("grad_state_own", 1, 0, ())
    grad, states, total = grad_state("grad_state", n_head - 1, 1, (total, grad, states))
    suffix = other_segments(total, True, n_seq)

    chunk_rows = pl.BlockSpec((half, chunk, size), lambda c, j, i: (j, c, 0))
    query_grad, key_part, value_part = call(
        local_grad_kernel,
        (n_chunk, 2),
        [chunk_rows] * 4
        + [pl.BlockSpec((half, 1, size, size), lambda c, j, i: (j, c, 0, 0))]
        + other_specs,
        [pl.BlockSpec((chunk, heads, size), lambda c, j, i: (c, 0, 0)), chunk_rows, chunk_rows],
        [
            array((tok_rows, heads, size), BF16),
            array((heads, tok_rows, size), F32),
            array((heads, tok_rows, size), F32),
        ],
        [pltpu.VMEM((heads, chunk, size), BF16), pltpu.VMEM((heads, size, size), F32)],
        cost(7 * unit, 9 * full_bytes),
        "local_grad",
    )(place, *hbm(query, key, value, grad, before), *prefix)

    last_first = pl.BlockSpec((heads, chunk, size), lambda c, i: (0, n_chunk - 1 - c, 0))
    tokens_last_first = pl.BlockSpec((chunk, heads, size), lambda c, i: (n_chunk - 1 - c, 0, 0))
    key_grad, value_grad = call(
        later_grad_kernel,
        (n_chunk,),
        [last_first] * 4
        + [pl.BlockSpec((1, heads, size, size), lambda c, i: (n_chunk - 1 - c, 0, 0, 0))]
        + other_specs,
        [tokens_last_first] * 2,
        [array((tok_rows, heads, size), BF16)] * 2,
        [pltpu.VMEM((heads, size, size), F32)] + [pltpu.VMEM((heads, chunk, size), BF16)] * 2,
        cost(2 * unit, 8 * full_bytes),
        "later_grad",
    )(place, *hbm(key, value), key_part, value_part, *hbm(states), *suffix)

    for steps in (order[:1], order[1:]) if aligned else ():
        if steps:
            attended = call(
                lambda *refs, steps=steps: place_kernel(steps, heads, *refs),
                (1,),
                [in_vmem] * len(steps) + [any_spec],
                any_spec,
                array(attended.shape, BF16),
                [pltpu.SemaphoreType.DMA((len(steps),))],
                cost(0, 4 * chunk * heads * size * len(steps)),
                "place",
                {1 + len(steps): 0},
            )(place, *[arrived[r] for r in steps], attended)
    if not aligned:
        own, attended = attended, jnp.zeros((chunk, heads * n_head, size), BF16)
        for r in [0] + order:
            part = arrived[r] if r else own
            attended = lax.dynamic_update_slice_in_dim(attended, part, (me ^ r) * heads, 1)
    return attended, query_grad, key_grad, value_grad


def solution(mesh):
    n_seq, n_head = mesh.shape["seq"], mesh.shape["head"]

    def body(*args):
        return per_device(n_seq, n_head, *args)

    return jax.shard_map(
        body,
        mesh=mesh,
        in_specs=(
            P("seq", "head", None),
            P("seq", "head", None),
            P("seq", "head", None),
            P(("seq", "head"), None, None),
        ),
        out_specs=(
            P(("seq", "head"), None, None),
            P("seq", "head", None),
            P("seq", "head", None),
            P("seq", "head", None),
        ),
        check_vma=False,
    )
```

time: 149 us -> 140 us (0.940)
  the two profiles are of different devices: /device:TPU:14 before, /device:TPU:12 now
where the time goes in v2:
time: 140 us; the launch traced here: 139 us
  waiting for transfers between devices  62.9 us (45%)
  Pallas kernels  53.9 us (38%)
  starting transfers between devices  18.6 us (13%)
  local copies, waits for them, and re-layouts  2.74 us (2%)
    ppermute x3, waiting for transfers between devices, per_device(): lax.ppermute(picked[r], 'head', [(i, i ^ r) for i in range(n_head)])  33.9 us
    ppermute x3, waiting for transfers between devices, per_device(): lax.ppermute(parts[r - 1], 'head', [(i, i ^ r) for i in range(n_head)])  27.7 us
    pallas_call x1, Pallas kernels, per_device(): call(local_grad_kernel, (n_chunk, 2), [chunk_rows] * 4 + [pl.BlockSpec((h...  16 us
    pallas_call x1, Pallas kernels, per_device(): call(lambda *refs: attended_kernel(n_head, *refs), (n_head, 2), [rows_spe...  11.2 us
    ppermute x6, starting transfers between devices, other_segments(): acc = acc + lax.ppermute(mine, 'seq', hops)  10.7 us
    pallas_call x1, Pallas kernels, per_device(): call(later_grad_kernel, (n_chunk,), [last_first] * 4 + [pl.BlockSpec((1,...  6.57 us
    pallas_call x2, Pallas kernels, grad_state(): call(lambda *refs: grad_state_kernel(count, *refs[:3 + count], *refs[3 +...  6.48 us
    pallas_call x1, Pallas kernels, per_device(): pl.pallas_call(key_state_kernel, grid=(n_chunk,), in_specs=[by_token, by_...  6.26 us
  transfers between devices with their start and end apart: 16, of which 5 were waited for; matrix products, arithmetic and copies ran while one was open for 2% of the time, Pallas kernels for 30%

profile of v2, /device:TPU:12, one launch (start us, length us, event | category | flops | bytes accessed | tf_op | source)
XLA Modules:
  0.0 139.3 jit_solution(5472839801073048123)
XLA Ops:
  0.6 6.3 %key_state.1 = (bf16[8,1024,128]{2,1,0:T(8,128)(2,1)}, bf16[8,1024,128]{2,1,0:T(8,128)(2,1)}, f32[8,4,128,128]{3,2,1,0:T(8,128)}, f32[8,128,128]{2,1,0:T(8,128)}) custom-call(bf16[1024,8,128]{2,1,0:T(8,128)(2,1)} %key_ref.1, bf16[1024,8,128]{2,1,0:T(8,128)(2,1)} %value_ref.1), custom_call_target="tpu_custom_call" | custom-call | flops 536870912 | bytes 10485760 | tf_op jit(solution)/shard_map/key_state/pallas_call | solution.py:256
  7.1 3.0 %shard_map.78 = (bf16[256,8,128]{2,1,0:T(8,128)(2,1)}, bf16[256,8,128]{2,1,0:T(8,128)(2,1)}, bf16[256,8,128]{2,1,0:T(8,128)(2,1)S(1)}) custom-call(s32[2]{0:T(128)S(1)} %pad_add_fusion.refs_0_.index_ref, bf16[256,32,128]{2,1,0:T(8,128)(2,1)} %refs_1_.3), custom_call_target="tpu_custom_call" | custom-call | bytes 3145728 | tf_op jit(solution)/shard_map/pallas_call | solution.py:224
  10.6 2.6 %collective-permute-start.9 = (bf16[256,8,128]{2,1,0:T(8,128)(2,1)}, bf16[256,8,128]{2,1,0:T(8,128)(2,1)S(1)}, u32[]{:S(2)}, u32[]{:S(2)}) collective-permute-start(bf16[256,8,128]{2,1,0:T(8,128)(2,1)} %get-tuple-element.35), channel_id=1, source_target_pairs={{0,2},{1,3},{2,0},{3,1},{4,6},{5,7},{6,4},{7,5},{8,10},{9,11},{10,... | collective-permute-start | bytes 1572872 | tf_op jit(solution)/shard_map/ppermute | solution.py:239
  13.2 1.6 %shard_map.79 = bf16[256,8,128]{2,1,0:T(8,128)(2,1)S(1)} custom-call(s32[2]{0:T(128)S(1)} %pad_add_fusion.refs_0_.index_ref, bf16[256,32,128]{2,1,0:T(8,128)(2,1)} %refs_1_.3), custom_call_target="tpu_custom_call" | custom-call | bytes 1048576 | tf_op jit(solution)/shard_map/pallas_call | solution.py:224
  15.3 1.7 %copy.14 = bf16[1024,8,128]{2,0,1:T(8,128)(2,1)} copy(bf16[1024,8,128]{2,1,0:T(8,128)(2,1)S(1)} %copy-done.2) | data formatting | bytes 4194304 | tf_op args[0]
  17.0 1.1 broadcast_in_dim.2.refs_5_.refs_2_
  18.0 2.2 %shard_map.80 = (bf16[8,1024,128]{2,1,0:T(8,128)(2,1)S(1)}, f32[4,8,128,128]{3,2,1,0:T(8,128)S(1)}, f32[8,128,128]{2,1,0:T(8,128)S(1)}) custom-call(s32[2]{0:T(128)S(1)} %pad_add_fusion.refs_0_.index_ref, bf16[8,1024,128]{2,1,0:T(8,128)(2,1)} %bitcast.5, f32[1024,128]{1,0:T(8,128)} %broadcast_in_dim.2.refs_5_.refs_2_, ...), custom_call_target="tpu_custom_call" | custom-call | flops 134217728 | bytes 2097152 | tf_op jit(solution)/shard_map/pallas_call | solution.py:306
  20.4 3.4 %collective-permute-start.3 = (f32[4,128,128]{2,1,0:T(8,128)S(1)}, f32[4,128,128]{2,1,0:T(8,128)S(1)}, u32[]{:S(2)}, u32[]{:S(2)}) collective-permute-start(f32[4,128,128]{2,1,0:T(8,128)S(1)} %dynamic-slice_add_fusion.1), channel_id=1, source_target_pairs={{0,8},{4,12},{8,16},{12,20},{16,24},{20,28},{1,9},{5,13},{9,17},{1... | collective-permute-start | bytes 786440 | tf_op jit(solution)/shard_map/ppermute | solution.py:180
  23.8 0.7 collective-permute-start.1
  24.5 9.1 %collective-permute-done.8.refs_3_ = bf16[256,8,128]{2,1,0:T(8,128)(2,1)S(1)} collective-permute-done((bf16[256,8,128]{2,1,0:T(8,128)(2,1)}, bf16[256,8,128]{2,1,0:T(8,128)(2,1)S(1)}, u32[]{:S(2)}, u32[]{:S(2)}) %collective-permute-start.8) | collective-permute-done | bytes 524320 | tf_op jit(solution)/shard_map/ppermute | solution.py:239
  33.6 1.3 collective-permute-start.2
  34.8 13.5 %collective-permute-done.9.refs_4_ = bf16[256,8,128]{2,1,0:T(8,128)(2,1)S(1)} collective-permute-done((bf16[256,8,128]{2,1,0:T(8,128)(2,1)}, bf16[256,8,128]{2,1,0:T(8,128)(2,1)S(1)}, u32[]{:S(2)}, u32[]{:S(2)}) %collective-permute-start.9) | collective-permute-done | bytes 524320 | tf_op jit(solution)/shard_map/ppermute | solution.py:239
  48.3 11.3 %collective-permute-done.10.refs_5_ = bf16[256,8,128]{2,1,0:T(8,128)(2,1)S(1)} collective-permute-done((bf16[256,8,128]{2,1,0:T(8,128)(2,1)S(1)}, bf16[256,8,128]{2,1,0:T(8,128)(2,1)S(1)}, u32[]{:S(2)}, u32[]{:S(2)}) %collective-permute-start.10) | collective-permute-done | bytes 524320 | tf_op jit(solution)/shard_map/ppermute | solution.py:239
  59.6 4.2 %shard_map.81 = (bf16[8,1024,128]{2,1,0:T(8,128)(2,1)S(1)}, f32[4,8,128,128]{3,2,1,0:T(8,128)S(1)}, f32[8,128,128]{2,1,0:T(8,128)S(1)}) custom-call(s32[2]{0:T(128)S(1)} %pad_add_fusion.refs_0_.index_ref, bf16[8,1024,128]{2,1,0:T(8,128)(2,1)} %bitcast.6, f32[1024,128]{1,0:T(8,128)} %broadcast_in_dim.2.refs_5_.refs_2_, ...), custom_call_target="tpu_custom_call", output_to_operand_aliasing={{0}: (7, {}), {1}: (8, {})} | custom-call | flops 402653184 | bytes 6291456 | tf_op jit(solution)/shard_map/pallas_call | solution.py:306
  64.6 1.3 collective-permute-done.11.refs_0_
  65.9 3.3 %collective-permute-start.14 = (f32[4,128,128]{2,1,0:T(8,128)S(1)}, f32[4,128,128]{2,1,0:T(8,128)S(1)}, u32[]{:S(2)}, u32[]{:S(2)}) collective-permute-start(f32[4,128,128]{2,1,0:T(8,128)S(1)} %dynamic-slice_add_fusion), channel_id=1, source_target_pairs={{8,0},{12,4},{16,8},{20,12},{24,16},{28,20},{9,1},{13,5},{17,9},{2... | collective-permute-start | bytes 786440 | tf_op jit(solution)/shard_map/ppermute | solution.py:180
  69.9 1.3 collective-permute-start.13
  71.3 11.2 %shard_map.75 = (bf16[256,8,128]{2,1,0:T(8,128)(2,1)S(1)}, bf16[256,8,128]{2,1,0:T(8,128)(2,1)S(1)}, bf16[256,8,128]{2,1,0:T(8,128)(2,1)S(1)}, bf16[256,32,128]{2,1,0:T(8,128)(2,1)}) custom-call(s32[2]{0:T(128)S(1)} %pad_add_fusion.refs_0_.index_ref, bf16[8,1024,128]{2,1,0:T(8,128)(2,1)} %bitcast.7, bf16[8,1024,128]{2,1,0:T(8,128)(2,1)} %get-tuple-element.26.refs_2_.key_ref, ...), custom_call_target="tpu_custom_call" | custom-call | flops 1610612736 | bytes 10485760 | tf_op jit(solution)/shard_map/pallas_call | solution.py:281
  82.5 3.0 %collective-permute-start.6 = (bf16[256,8,128]{2,1,0:T(8,128)(2,1)S(1)}, bf16[256,8,128]{2,1,0:T(8,128)(2,1)S(1)}, u32[]{:S(2)}, u32[]{:S(2)}) collective-permute-start(bf16[256,8,128]{2,1,0:T(8,128)(2,1)S(1)} %get-tuple-element.31), channel_id=1, source_target_pairs={{0,1},{1,0},{2,3},{3,2},{4,5},{5,4},{6,7},{7,6},{8,9},{9,8},{10,11... | collective-permute-start | bytes 1572872 | tf_op jit(solution)/shard_map/ppermute | solution.py:300
  86.1 16.0 %shard_map.82 = (bf16[1024,8,128]{2,1,0:T(8,128)(2,1)}, f32[8,1024,128]{2,1,0:T(8,128)S(1)}, f32[8,1024,128]{2,1,0:T(8,128)S(1)}) custom-call(s32[2]{0:T(128)S(1)} %pad_add_fusion.refs_0_.index_ref, bf16[8,1024,128]{2,1,0:T(8,128)(2,1)} %bitcast.8, bf16[8,1024,128]{2,1,0:T(8,128)(2,1)} %get-tuple-element.26.refs_2_.key_ref, ...), custom_call_target="tpu_custom_call" | custom-call | flops 3758096384 | bytes 18874368 | tf_op jit(solution)/shard_map/pallas_call | solution.py:332
  102.1 27.7 %collective-permute-done.7.refs_1_ = bf16[256,8,128]{2,1,0:T(8,128)(2,1)S(1)} collective-permute-done((bf16[256,8,128]{2,1,0:T(8,128)(2,1)S(1)}, bf16[256,8,128]{2,1,0:T(8,128)(2,1)S(1)}, u32[]{:S(2)}, u32[]{:S(2)}) %collective-permute-start.7) | collective-permute-done | bytes 524320 | tf_op jit(solution)/shard_map/ppermute | solution.py:300
  129.8 1.3 shard_map.76.refs_3_
  131.2 1.5 %shard_map.77 = bf16[256,32,128]{2,1,0:T(8,128)(2,1)} custom-call(s32[2]{0:T(128)S(1)} %pad_add_fusion.refs_0_.index_ref, bf16[256,8,128]{2,1,0:T(8,128)(2,1)S(1)} %collective-permute-done.5.refs_1_, bf16[256,8,128]{2,1,0:T(8,128)(2,1)S(1)} %collective-permute-done.6.refs_2_, bf16[256,32,128]{2,1,0:T(8,128)(2,1)} %shard_map.76.refs_3_), custom_call_target="tpu_custom_call", output_to_operand_aliasing={{}: (3, {})} | custom-call | bytes 2097152 | tf_op jit(solution)/shard_map/pallas_call | solution.py:366
  132.7 6.6 %shard_map.83 = (bf16[1024,8,128]{2,1,0:T(8,128)(2,1)}, bf16[1024,8,128]{2,1,0:T(8,128)(2,1)}) custom-call(s32[2]{0:T(128)S(1)} %pad_add_fusion.refs_0_.index_ref, bf16[8,1024,128]{2,1,0:T(8,128)(2,1)} %get-tuple-element.26.refs_2_.key_ref, bf16[8,1024,128]{2,1,0:T(8,128)(2,1)} %get-tuple-element.27.refs_3_.value_ref, ...), custom_call_target="tpu_custom_call" | custom-call | flops 1073741824 | bytes 16777216 | tf_op jit(solution)/shard_map/pallas_call | solution.py:351
  (34 shorter events, 3.3 us)
Async XLA Ops:
  6.9 13.4 %collective-permute-start = (f32[8,128,128]{2,1,0:T(8,128)}, f32[8,128,128]{2,1,0:T(8,128)S(1)}, u32[]{:S(2)}, u32[]{:S(2)}) collective-permute-start(f32[8,128,128]{2,1,0:T(8,128)} %get-tuple-element.29), channel_id=1, source_target_pairs={{0,4},{4,0},{8,12},{12,8},{16,20},{20,16},{24,28},{28,24},{1,5},{5... | collective-permute-start | bytes 1572872 | tf_op jit(solution)/shard_map/ppermute | solution.py:173
  7.1 8.3 %copy-start.2 = (bf16[1024,8,128]{2,1,0:T(8,128)(2,1)S(1)}, bf16[1024,8,128]{2,1,0:T(8,128)(2,1)}, u32[]{:S(2)}) copy-start(bf16[1024,8,128]{2,1,0:T(8,128)(2,1)} %param.4) | copy-start | bytes 6291460
  10.1 23.5 %collective-permute-start.8 = (bf16[256,8,128]{2,1,0:T(8,128)(2,1)}, bf16[256,8,128]{2,1,0:T(8,128)(2,1)S(1)}, u32[]{:S(2)}, u32[]{:S(2)}) collective-permute-start(bf16[256,8,128]{2,1,0:T(8,128)(2,1)} %get-tuple-element.34), channel_id=1, source_target_pairs={{0,1},{1,0},{2,3},{3,2},{4,5},{5,4},{6,7},{7,6},{8,9},{9,8},{10,11... | collective-permute-start | bytes 1572872 | tf_op jit(solution)/shard_map/ppermute | solution.py:239
  10.6 37.7 %collective-permute-start.9 = (bf16[256,8,128]{2,1,0:T(8,128)(2,1)}, bf16[256,8,128]{2,1,0:T(8,128)(2,1)S(1)}, u32[]{:S(2)}, u32[]{:S(2)}) collective-permute-start(bf16[256,8,128]{2,1,0:T(8,128)(2,1)} %get-tuple-element.35), channel_id=1, source_target_pairs={{0,2},{1,3},{2,0},{3,1},{4,6},{5,7},{6,4},{7,5},{8,10},{9,11},{10,... | collective-permute-start | bytes 1572872 | tf_op jit(solution)/shard_map/ppermute | solution.py:239
  14.8 44.8 %collective-permute-start.10 = (bf16[256,8,128]{2,1,0:T(8,128)(2,1)S(1)}, bf16[256,8,128]{2,1,0:T(8,128)(2,1)S(1)}, u32[]{:S(2)}, u32[]{:S(2)}) collective-permute-start(bf16[256,8,128]{2,1,0:T(8,128)(2,1)S(1)} %shard_map.79), channel_id=1, source_target_pairs={{0,3},{1,2},{2,1},{3,0},{4,7},{5,6},{6,5},{7,4},{8,11},{9,10},{10,... | collective-permute-start | bytes 1572872 | tf_op jit(solution)/shard_map/ppermute | solution.py:239
  17.0 3.3 %copy-start.3 = (f32[8,128,128]{2,1,0:T(8,128)S(1)}, f32[8,128,128]{2,1,0:T(8,128)}, u32[]{:S(2)}) copy-start(f32[8,128,128]{2,1,0:T(8,128)} %get-tuple-element.29) | copy-start | bytes 1572868
  20.4 43.6 %collective-permute-start.3 = (f32[4,128,128]{2,1,0:T(8,128)S(1)}, f32[4,128,128]{2,1,0:T(8,128)S(1)}, u32[]{:S(2)}, u32[]{:S(2)}) collective-permute-start(f32[4,128,128]{2,1,0:T(8,128)S(1)} %dynamic-slice_add_fusion.1), channel_id=1, source_target_pairs={{0,8},{4,12},{8,16},{12,20},{16,24},{20,28},{1,9},{5,13},{9,17},{1... | collective-permute-start | bytes 786440 | tf_op jit(solution)/shard_map/ppermute | solution.py:180
  23.8 40.2 %collective-permute-start.1 = (f32[4,128,128]{2,1,0:T(8,128)S(1)}, f32[4,128,128]{2,1,0:T(8,128)S(1)}, u32[]{:S(2)}, u32[]{:S(2)}) collective-permute-start(f32[4,128,128]{2,1,0:T(8,128)S(1)} %dynamic-slice_add_fusion.1), channel_id=1, source_target_pairs={{0,24},{4,28},{1,25},{5,29},{2,26},{6,30},{3,27},{7,31}} | collective-permute-start | bytes 786440 | tf_op jit(solution)/shard_map/ppermute | solution.py:180
  33.6 30.4 %collective-permute-start.2 = (f32[4,128,128]{2,1,0:T(8,128)S(1)}, f32[4,128,128]{2,1,0:T(8,128)S(1)}, u32[]{:S(2)}, u32[]{:S(2)}) collective-permute-start(f32[4,128,128]{2,1,0:T(8,128)S(1)} %dynamic-slice_add_fusion.1), channel_id=1, source_target_pairs={{0,16},{4,20},{8,24},{12,28},{1,17},{5,21},{9,25},{13,29},{2,18},{... | collective-permute-start | bytes 786440 | tf_op jit(solution)/shard_map/ppermute | solution.py:180
  63.9 18.6 %copy-start = (f32[4,8,128,128]{3,2,1,0:T(8,128)}, f32[4,8,128,128]{3,2,1,0:T(8,128)S(1)}, u32[]{:S(2)}) copy-start(f32[4,8,128,128]{3,2,1,0:T(8,128)S(1)} %get-tuple-element.44.state_ref) | copy-start | bytes 6291460
  63.9 18.6 %copy-start.1 = (bf16[8,1024,128]{2,1,0:T(8,128)(2,1)}, bf16[8,1024,128]{2,1,0:T(8,128)(2,1)S(1)}, u32[]{:S(2)}) copy-start(bf16[8,1024,128]{2,1,0:T(8,128)(2,1)S(1)} %get-tuple-element.40.grad_ref) | copy-start | bytes 6291460
  63.9 2.0 %collective-permute-start.11 = (f32[8,128,128]{2,1,0:T(8,128)S(1)}, f32[8,128,128]{2,1,0:T(8,128)S(1)}, u32[]{:S(2)}, u32[]{:S(2)}) collective-permute-start(f32[8,128,128]{2,1,0:T(8,128)S(1)} %get-tuple-element.45), channel_id=1, source_target_pairs={{0,4},{4,0},{8,12},{12,8},{16,20},{20,16},{24,28},{28,24},{1,5},{5... | collective-permute-start | bytes 1572872 | tf_op jit(solution)/shard_map/ppermute | solution.py:173
  64.0 7.2 %collective-permute-start.4 = (f32[4,128,128]{2,1,0:T(8,128)S(1)}, f32[4,128,128]{2,1,0:T(8,128)S(1)}, u32[]{:S(2)}, u32[]{:S(2)}) collective-permute-start(f32[4,128,128]{2,1,0:T(8,128)S(1)} %add_add_fusion.1.refs_7_.refs_1_), channel_id=1, source_target_pairs={{0,4},{4,0},{8,12},{12,8},{16,20},{20,16},{24,28},{28,24},{1,5},{5... | collective-permute-start | bytes 786440 | tf_op jit(solution)/shard_map/ppermute | solution.py:181
  65.9 19.7 %collective-permute-start.14 = (f32[4,128,128]{2,1,0:T(8,128)S(1)}, f32[4,128,128]{2,1,0:T(8,128)S(1)}, u32[]{:S(2)}, u32[]{:S(2)}) collective-permute-start(f32[4,128,128]{2,1,0:T(8,128)S(1)} %dynamic-slice_add_fusion), channel_id=1, source_target_pairs={{8,0},{12,4},{16,8},{20,12},{24,16},{28,20},{9,1},{13,5},{17,9},{2... | collective-permute-start | bytes 786440 | tf_op jit(solution)/shard_map/ppermute | solution.py:180
  69.2 16.8 %collective-permute-start.12 = (f32[4,128,128]{2,1,0:T(8,128)S(1)}, f32[4,128,128]{2,1,0:T(8,128)S(1)}, u32[]{:S(2)}, u32[]{:S(2)}) collective-permute-start(f32[4,128,128]{2,1,0:T(8,128)S(1)} %dynamic-slice_add_fusion), channel_id=1, source_target_pairs={{24,0},{28,4},{25,1},{29,5},{26,2},{30,6},{27,3},{31,7}} | collective-permute-start | bytes 786440 | tf_op jit(solution)/shard_map/ppermute | solution.py:180
  69.9 16.1 %collective-permute-start.13 = (f32[4,128,128]{2,1,0:T(8,128)S(1)}, f32[4,128,128]{2,1,0:T(8,128)S(1)}, u32[]{:S(2)}, u32[]{:S(2)}) collective-permute-start(f32[4,128,128]{2,1,0:T(8,128)S(1)} %dynamic-slice_add_fusion), channel_id=1, source_target_pairs={{16,0},{20,4},{24,8},{28,12},{17,1},{21,5},{25,9},{29,13},{18,2},{... | collective-permute-start | bytes 786440 | tf_op jit(solution)/shard_map/ppermute | solution.py:180
  82.4 48.7 %collective-permute-start.5 = (bf16[256,8,128]{2,1,0:T(8,128)(2,1)S(1)}, bf16[256,8,128]{2,1,0:T(8,128)(2,1)S(1)}, u32[]{:S(2)}, u32[]{:S(2)}) collective-permute-start(bf16[256,8,128]{2,1,0:T(8,128)(2,1)S(1)} %get-tuple-element.30), channel_id=1, source_target_pairs={{0,2},{1,3},{2,0},{3,1},{4,6},{5,7},{6,4},{7,5},{8,10},{9,11},{10,... | collective-permute-start | bytes 1572872 | tf_op jit(solution)/shard_map/ppermute | solution.py:300
  82.5 48.6 %collective-permute-start.6 = (bf16[256,8,128]{2,1,0:T(8,128)(2,1)S(1)}, bf16[256,8,128]{2,1,0:T(8,128)(2,1)S(1)}, u32[]{:S(2)}, u32[]{:S(2)}) collective-permute-start(bf16[256,8,128]{2,1,0:T(8,128)(2,1)S(1)} %get-tuple-element.31), channel_id=1, source_target_pairs={{0,1},{1,0},{2,3},{3,2},{4,5},{5,4},{6,7},{7,6},{8,9},{9,8},{10,11... | collective-permute-start | bytes 1572872 | tf_op jit(solution)/shard_map/ppermute | solution.py:300
  85.5 44.3 %collective-permute-start.7 = (bf16[256,8,128]{2,1,0:T(8,128)(2,1)S(1)}, bf16[256,8,128]{2,1,0:T(8,128)(2,1)S(1)}, u32[]{:S(2)}, u32[]{:S(2)}) collective-permute-start(bf16[256,8,128]{2,1,0:T(8,128)(2,1)S(1)} %get-tuple-element.32), channel_id=1, source_target_pairs={{0,3},{1,2},{2,1},{3,0},{4,7},{5,6},{6,5},{7,4},{8,11},{9,10},{10,... | collective-permute-start | bytes 1572872 | tf_op jit(solution)/shard_map/ppermute | solution.py:300
  86.0 46.7 %collective-permute-start.15 = (f32[4,128,128]{2,1,0:T(8,128)S(1)}, f32[4,128,128]{2,1,0:T(8,128)S(1)}, u32[]{:S(2)}, u32[]{:S(2)}) collective-permute-start(f32[4,128,128]{2,1,0:T(8,128)S(1)} %add_add_fusion.refs_1_), channel_id=1, source_target_pairs={{0,4},{4,0},{8,12},{12,8},{16,20},{20,16},{24,28},{28,24},{1,5},{5... | collective-permute-start | bytes 786440 | tf_op jit(solution)/shard_map/ppermute | solution.py:181

commit v3 on v2

--- a/solution.py
+++ b/solution.py
@@ -9,7 +9,7 @@
 F32 = jnp.float32
 BF16 = jnp.bfloat16
 VMEM_LIMIT = 20 * 1024 * 1024
-IN_VMEM = ('place', 'pick', 'local_grad', 'later_grad', 'grad_state', 'grad_state_own', 'attended')
+IN_VMEM = ('place', 'pick', 'local_grad_early', 'local_grad_last', 'later_grad', 'grad_state_early', 'grad_state_last', 'attended')
 
 
 def dot(lhs, rhs, lhs_dim, rhs_dim):
@@ -39,6 +39,14 @@
     total_ref[...] = running[...]
 
 
+def query_layout_kernel(index_ref, query_ref, query_out, scale_ref):
+    rows, size = scale_ref.shape
+    first = (index_ref[2] * pl.num_programs(0) + pl.program_id(0)) * rows
+    position = (first + lax.broadcasted_iota(jnp.int32, (rows, size), 0)).astype(F32)
+    scale_ref[...] = 1.0 / jnp.sqrt(size * (position + 1.0))
+    query_out[...] = jnp.swapaxes(query_ref[...], 0, 1)
+
+
 def base_state(held_refs, core, j, later, half, h):
     twin_ref, mine_ref, theirs_ref = held_refs
     use_twin = core == (0 if later else 1)
@@ -47,26 +55,26 @@
 
 
 def attended_kernel(n_head, index_ref, query_ref, key_ref, value_ref, before_ref, scale_ref, *refs):
-    prefix_refs, outs, held, base = refs[:3], refs[3:-2], refs[-2], refs[-1]
-    r, j = pl.program_id(0), pl.program_id(1)
-    half, rows = query_ref.shape[:2]
+    prefix_refs, outs, held, base, scores = refs[:3], refs[3:-3], refs[-3], refs[-2], refs[-1]
+    r = pl.program_id(0)
+    heads, rows = query_ref.shape[:2]
     mask = iota(rows, 1) <= iota(rows, 0)
     scale = scale_ref[...]
 
     @pl.when(r == 0)
     def _():
-        for h in range(half):
-            base[j * half + h] = base_state(prefix_refs, index_ref[1], j, False, half, h)
-
-    for h in range(half):
-        query = query_ref[h]
-        state = (base[j * half + h] + before_ref[h, 0]).astype(BF16)
-        within = masked(mask, dot(query, key_ref[h], 1, 1))
-        total = dot(query, state, 1, 0) + dot(within, value_ref[h], 1, 0)
-        held[j * half + h] = (scale * total).astype(BF16)
+        for h in range(heads):
+            base[h] = base_state(prefix_refs, index_ref[1], h // (heads // 2), False, heads // 2, h % (heads // 2))
+
+    for h in range(heads):
+        scores[h] = masked(mask, dot(query_ref[h], key_ref[h], 1, 1))
+    for h in range(heads):
+        state = (base[h] + before_ref[h, 0]).astype(BF16)
+        total = dot(query_ref[h], state, 1, 0) + dot(scores[h], value_ref[h], 1, 0)
+        held[h] = (scale * total).astype(BF16)
     for step in range(n_head):
 
-        @pl.when((j == 1) & (r == step))
+        @pl.when(r == step)
         def _():
             outs[step - 1][...] = jnp.swapaxes(held[...], 0, 1)
 
@@ -162,6 +170,10 @@
         copy.wait()
 
 
+def send_order(n_head):
+    return [n_head - 1, *range(1, n_head - 1)]
+
+
 def cost(flops, size):
     return pl.CostEstimate(flops=int(flops), bytes_accessed=int(size), transcendentals=0)
 
@@ -172,12 +184,14 @@
     swap = [(i, i ^ 1) for i in range(n_seq)]
     twin = lax.ppermute(total, "seq", swap)
     mine = lax.dynamic_slice_in_dim(total + twin, core * half, half, 0)
-    acc = jnp.zeros_like(mine)
+    if not later:
+        mine = mine.astype(BF16)
+    acc = jnp.zeros(mine.shape, F32)
     for step in range(n_seq // 2 - 1, 0, -1):
         hops = [(i, i + 2 * step) for i in range(n_seq - 2 * step)]
         if later:
             hops = [(b, a) for a, b in hops]
-        acc = acc + lax.ppermute(mine, "seq", hops)
+        acc = acc + lax.ppermute(mine, "seq", hops).astype(F32)
     theirs = lax.ppermute(acc, "seq", swap)
     return twin, acc, theirs
 
@@ -187,10 +201,11 @@
     chunk = out_grad.shape[0]
     n_chunk = tok_rows // chunk
     me = lax.axis_index("head")
-    order = sorted(range(1, n_head), reverse=True)
+    order = send_order(n_head)
     array = jax.ShapeDtypeStruct
     core = lax.axis_index("seq") % 2
-    place = jnp.stack([me, core]).astype(jnp.int32)
+    proc = [0] + order
+    place = jnp.stack([me, core, lax.axis_index("seq")] + [me ^ r for r in proc]).astype(jnp.int32)
     any_spec = pl.BlockSpec(memory_space=pl.ANY)
 
     def call(kernel, grid, in_specs, out_specs, out_shape, scratch, estimate, name, aliases={}):
@@ -238,10 +253,6 @@
     for r in order:
         pieces[r] = lax.ppermute(picked[r], "head", [(i, i ^ r) for i in range(n_head)])
     pieces[0] = picked[0]
-
-    position = (lax.axis_index("seq") * tok_rows + lax.iota(jnp.int32, tok_rows)).astype(F32)
-    scaling = 1.0 / jnp.sqrt(size * (position + 1.0))
-    scale = jnp.broadcast_to(scaling[:, None], (tok_rows, size))
 
     full_bytes = heads * tok_rows * size * 2
     unit = 2 * heads * tok_rows * size * chunk
@@ -268,40 +279,46 @@
         cost_estimate=cost(unit, 5 * full_bytes),
         name="key_state",
     )(key_vectors, value_vectors)
-    query = jnp.transpose(queries, (1, 0, 2))
+    query, scale = call(
+        query_layout_kernel,
+        (n_chunk,),
+        [by_token],
+        [by_head, pl.BlockSpec((chunk, size), lambda c, i: (c, 0))],
+        [head_shape, array((tok_rows, size), F32)],
+        [],
+        cost(unit // 4, 2 * full_bytes),
+        "query_layout",
+    )(place, *hbm(queries))
     prefix = other_segments(key_total, False, n_seq)
 
     half_states = pl.BlockSpec((half, size, size), lambda *_: (0, 0, 0))
     other_specs = [all_states, half_states, half_states]
 
-    def rows_of(r, j, i):
-        return (j, i[0] ^ r, 0)
-
-    rows_spec = pl.BlockSpec((half, chunk, size), rows_of)
+    rows_spec = pl.BlockSpec((heads, chunk, size), lambda r, i: (0, i[3 + r], 0))
     *parts, attended = call(
         lambda *refs: attended_kernel(n_head, *refs),
-        (n_head, 2),
+        (n_head,),
         [rows_spec] * 3
         + [
-            pl.BlockSpec((half, 1, size, size), lambda r, j, i: (j, i[0] ^ r, 0, 0)),
-            pl.BlockSpec((chunk, size), lambda r, j, i: (i[0] ^ r, 0)),
+            pl.BlockSpec((heads, 1, size, size), lambda r, i: (0, i[3 + r], 0, 0)),
+            pl.BlockSpec((chunk, size), lambda r, i: (i[3 + r], 0)),
         ]
         + other_specs,
         [whole_piece] * (n_head - 1)
-        + ([pl.BlockSpec((chunk, heads, size), lambda r, j, i: (0, i[0], 0))] if aligned else [whole_piece]),
+        + ([pl.BlockSpec((chunk, heads, size), lambda r, i: (0, i[0], 0))] if aligned else [whole_piece]),
         [piece_shape] * (n_head - 1)
         + ([array((chunk, heads * n_head, size), BF16)] if aligned else [piece_shape]),
-        [pltpu.VMEM((heads, chunk, size), BF16), pltpu.VMEM((heads, size, size), F32)],
+        [pltpu.VMEM((heads, chunk, size), BF16), pltpu.VMEM((heads, size, size), F32), pltpu.VMEM((heads, chunk, chunk), BF16)],
         cost(3 * unit, 5 * full_bytes),
         "attended",
     )(place, *hbm(query, key, value, before, scale), *prefix)
     arrived = {}
     for r in order:
-        arrived[r] = lax.ppermute(parts[r - 1], "head", [(i, i ^ r) for i in range(n_head)])
+        arrived[r] = lax.ppermute(parts[proc.index(r) - 1], "head", [(i, i ^ r) for i in range(n_head)])
 
     def grad_state(name, count, first, extra):
         def at(step, i):
-            return i[0] ^ (step + first)
+            return i[3 + first + step]
 
         return call(
             lambda *refs: grad_state_kernel(count, *refs[: 3 + count], *refs[3 + count : -3][:1], *refs[-3:]),
@@ -317,34 +334,45 @@
                 pl.BlockSpec((1, heads, size, size), lambda s, i: (at(s, i), 0, 0, 0)),
                 all_states,
             ],
-            [head_shape, states_shape, state_shape],
+            [pltpu.HBM(head_shape.shape, BF16), pltpu.HBM(states_shape.shape, F32), state_shape],
             [],
             cost(unit * count // n_chunk, 4 * full_bytes * count // n_chunk),
             name,
             {4 + count: 0, 5 + count: 1} if extra else {},
-        )(place, *hbm(query, scale), *[pieces[first + k] for k in range(count)], *extra)
-
-    grad, states, total = grad_state("grad_state_own", 1, 0, ())
-    grad, states, total = grad_state("grad_state", n_head - 1, 1, (total, grad, states))
+        )(place, *hbm(query, scale), *[pieces[r] for r in proc[first : first + count]], *extra)
+
+    early = n_head
+    grad, states, total = grad_state("grad_state_early", early, 0, ())
+    early_grad = grad
+    if early < n_head:
+        grad, states, total = grad_state("grad_state_last", n_head - early, early, (total, grad, states))
     suffix = other_segments(total, True, n_seq)
 
-    chunk_rows = pl.BlockSpec((half, chunk, size), lambda c, j, i: (j, c, 0))
-    query_grad, key_part, value_part = call(
-        local_grad_kernel,
-        (n_chunk, 2),
-        [chunk_rows] * 4
-        + [pl.BlockSpec((half, 1, size, size), lambda c, j, i: (j, c, 0, 0))]
-        + other_specs,
-        [pl.BlockSpec((chunk, heads, size), lambda c, j, i: (c, 0, 0)), chunk_rows, chunk_rows],
-        [
-            array((tok_rows, heads, size), BF16),
-            array((heads, tok_rows, size), F32),
-            array((heads, tok_rows, size), F32),
-        ],
-        [pltpu.VMEM((heads, chunk, size), BF16), pltpu.VMEM((heads, size, size), F32)],
-        cost(7 * unit, 9 * full_bytes),
-        "local_grad",
-    )(place, *hbm(query, key, value, grad, before), *prefix)
+    def local_grad(name, count, first, grad, outs):
+        chunk_rows = pl.BlockSpec((half, chunk, size), lambda c, j, i: (j, i[3 + first + c], 0))
+        return call(
+            lambda *refs: local_grad_kernel(*refs[:9], *refs[9 + len(outs) :]),
+            (count, 2),
+            [chunk_rows] * 4
+            + [pl.BlockSpec((half, 1, size, size), lambda c, j, i: (j, i[3 + first + c], 0, 0))]
+            + other_specs
+            + [any_spec] * len(outs),
+            [pl.BlockSpec((chunk, heads, size), lambda c, j, i: (i[3 + first + c], 0, 0)), chunk_rows, chunk_rows],
+            [
+                array((tok_rows, heads, size), BF16),
+                array((heads, tok_rows, size), F32),
+                array((heads, tok_rows, size), F32),
+            ],
+            [pltpu.VMEM((heads, chunk, size), BF16), pltpu.VMEM((heads, size, size), F32)],
+            cost(7 * unit * count // n_chunk, 9 * full_bytes * count // n_chunk),
+            name,
+            {9 + k: k for k in range(len(outs))},
+        )(place, *hbm(query, key, value, grad, before), *prefix, *outs)
+
+    outs = local_grad("local_grad_early", early, 0, early_grad, ())
+    if early < n_head:
+        outs = local_grad("local_grad_last", n_head - early, early, grad, outs)
+    query_grad, key_part, value_part = outs
 
     last_first = pl.BlockSpec((heads, chunk, size), lambda c, i: (0, n_chunk - 1 - c, 0))
     tokens_last_first = pl.BlockSpec((chunk, heads, size), lambda c, i: (n_chunk - 1 - c, 0, 0))
@@ -361,7 +389,7 @@
         "later_grad",
     )(place, *hbm(key, value), key_part, value_part, *hbm(states), *suffix)
 
-    for steps in (order[:1], order[1:]) if aligned else ():
+    for steps in (order[:-1], order[-1:]) if aligned else ():
         if steps:
             attended = call(
                 lambda *refs, steps=steps: place_kernel(steps, heads, *refs),

time: 140 us -> 141 us (level)
  the two profiles are of different devices: /device:TPU:12 before, /device:TPU:15 now
where the time goes in v3:
time: 141 us; the launch traced here: 140 us
  waiting for transfers between devices  61.3 us (43%)
  Pallas kernels  55.5 us (39%)
  starting transfers between devices  21 us (15%)
    ppermute x3, waiting for transfers between devices, per_device(): lax.ppermute(parts[proc.index(r) - 1], 'head', [(i, i ^ r) for i in range...  27.2 us
    ppermute x3, waiting for transfers between devices, per_device(): lax.ppermute(picked[r], 'head', [(i, i ^ r) for i in range(n_head)])  26.9 us
    pallas_call x1, Pallas kernels, local_grad(): call(lambda *refs: local_grad_kernel(*refs[:9], *refs[9 + len(outs):]), (...  16.5 us
    ppermute x6, starting transfers between devices, other_segments(): acc = acc + lax.ppermute(mine, 'seq', hops).astype(F32)  7.97 us
    pallas_call x1, Pallas kernels, per_device(): call(lambda *refs: attended_kernel(n_head, *refs), (n_head,), [rows_spec]...  7.66 us
    ppermute x6, waiting for transfers between devices, other_segments(): acc = acc + lax.ppermute(mine, 'seq', hops).astype(F32)  7.17 us
    pallas_call x1, Pallas kernels, per_device(): call(later_grad_kernel, (n_chunk,), [last_first] * 4 + [pl.BlockSpec((1,...  6.56 us
    pallas_call x1, Pallas kernels, grad_state(): call(lambda *refs: grad_state_kernel(count, *refs[:3 + count], *refs[3 +...  6.38 us
  transfers between devices with their start and end apart: 16, of which 7 were waited for; matrix products, arithmetic and copies ran while one was open for 1% of the time, Pallas kernels for 34%

profile of v3, /device:TPU:15, one launch (start us, length us, event | category | flops | bytes accessed | tf_op | source)
XLA Modules:
  0.0 139.8 jit_solution(16925352968741827047)
XLA Ops:
  0.7 1.6 %shard_map.80 = bf16[256,8,128]{2,1,0:T(8,128)(2,1)S(1)} custom-call(s32[7]{0:T(128)S(1)} %stack.28.index_ref.refs_0_, bf16[256,32,128]{2,1,0:T(8,128)(2,1)} %refs_1_.3), custom_call_target="tpu_custom_call" | custom-call | bytes 1048576 | tf_op jit(solution)/shard_map/pallas_call | solution.py:239
  2.3 1.4 collective-permute-start.8
  3.7 3.0 %shard_map.79 = (bf16[256,8,128]{2,1,0:T(8,128)(2,1)}, bf16[256,8,128]{2,1,0:T(8,128)(2,1)}, bf16[256,8,128]{2,1,0:T(8,128)(2,1)S(1)}) custom-call(s32[7]{0:T(128)S(1)} %stack.28.index_ref.refs_0_, bf16[256,32,128]{2,1,0:T(8,128)(2,1)} %refs_1_.3), custom_call_target="tpu_custom_call" | custom-call | bytes 3145728 | tf_op jit(solution)/shard_map/pallas_call | solution.py:239
  6.7 2.3 %collective-permute-start.9 = (bf16[256,8,128]{2,1,0:T(8,128)(2,1)}, bf16[256,8,128]{2,1,0:T(8,128)(2,1)S(1)}, u32[]{:S(2)}, u32[]{:S(2)}) collective-permute-start(bf16[256,8,128]{2,1,0:T(8,128)(2,1)} %get-tuple-element.36), channel_id=1, source_target_pairs={{0,1},{1,0},{2,3},{3,2},{4,5},{5,4},{6,7},{7,6},{8,9},{9,8},{10,11... | collective-permute-start | bytes 1572872 | tf_op jit(solution)/shard_map/ppermute | solution.py:254
  8.9 6.3 %key_state.1 = (bf16[8,1024,128]{2,1,0:T(8,128)(2,1)}, bf16[8,1024,128]{2,1,0:T(8,128)(2,1)}, f32[8,4,128,128]{3,2,1,0:T(8,128)}, f32[8,128,128]{2,1,0:T(8,128)}) custom-call(bf16[1024,8,128]{2,1,0:T(8,128)(2,1)} %key_ref.1, bf16[1024,8,128]{2,1,0:T(8,128)(2,1)} %value_ref.1), custom_call_target="tpu_custom_call" | custom-call | flops 536870912 | bytes 10485760 | tf_op jit(solution)/shard_map/key_state/pallas_call | solution.py:267
  16.5 4.7 %shard_map.75 = (bf16[8,1024,128]{2,1,0:T(8,128)(2,1)}, f32[1024,128]{1,0:T(8,128)}) custom-call(s32[7]{0:T(128)} %copy-done, bf16[1024,8,128]{2,1,0:T(8,128)(2,1)} %query_ref.1), custom_call_target="tpu_custom_call" | custom-call | flops 134217728 | bytes 4194304 | tf_op jit(solution)/shard_map/pallas_call | solution.py:282
  21.2 5.4 %collective-permute-done.8.refs_4_ = bf16[256,8,128]{2,1,0:T(8,128)(2,1)S(1)} collective-permute-done((bf16[256,8,128]{2,1,0:T(8,128)(2,1)S(1)}, bf16[256,8,128]{2,1,0:T(8,128)(2,1)S(1)}, u32[]{:S(2)}, u32[]{:S(2)}) %collective-permute-start.8) | collective-permute-done | bytes 524320 | tf_op jit(solution)/shard_map/ppermute | solution.py:254
  26.6 2.0 %collective-permute-done.9.refs_5_ = bf16[256,8,128]{2,1,0:T(8,128)(2,1)S(1)} collective-permute-done((bf16[256,8,128]{2,1,0:T(8,128)(2,1)}, bf16[256,8,128]{2,1,0:T(8,128)(2,1)S(1)}, u32[]{:S(2)}, u32[]{:S(2)}) %collective-permute-start.9) | collective-permute-done | bytes 524320 | tf_op jit(solution)/shard_map/ppermute | solution.py:254
  28.6 19.5 %collective-permute-done.10.refs_6_ = bf16[256,8,128]{2,1,0:T(8,128)(2,1)S(1)} collective-permute-done((bf16[256,8,128]{2,1,0:T(8,128)(2,1)}, bf16[256,8,128]{2,1,0:T(8,128)(2,1)S(1)}, u32[]{:S(2)}, u32[]{:S(2)}) %collective-permute-start.10) | collective-permute-done | bytes 524320 | tf_op jit(solution)/shard_map/ppermute | solution.py:254
  48.1 6.4 %shard_map.81 = (bf16[8,1024,128]{2,1,0:T(8,128)(2,1)}, f32[4,8,128,128]{3,2,1,0:T(8,128)}, f32[8,128,128]{2,1,0:T(8,128)S(1)}) custom-call(s32[7]{0:T(128)S(1)} %copy-done.1, bf16[8,1024,128]{2,1,0:T(8,128)(2,1)} %get-tuple-element.25.refs_1_, f32[1024,128]{1,0:T(8,128)} %get-tuple-element.29.refs_5_.refs_2_, ...), custom_call_target="tpu_custom_call" | custom-call | flops 536870912 | bytes 8388608 | tf_op jit(solution)/shard_map/pallas_call | solution.py:323
  54.5 1.5 %collective-permute-start.11 = (f32[8,128,128]{2,1,0:T(8,128)S(1)}, f32[8,128,128]{2,1,0:T(8,128)S(1)}, u32[]{:S(2)}, u32[]{:S(2)}) collective-permute-start(f32[8,128,128]{2,1,0:T(8,128)S(1)} %get-tuple-element.43), channel_id=1, source_target_pairs={{0,4},{4,0},{8,12},{12,8},{16,20},{20,16},{24,28},{28,24},{1,5},{5... | collective-permute-start | bytes 1572872 | tf_op jit(solution)/shard_map/ppermute | solution.py:185
  60.9 3.0 %collective-permute-done.3 = bf16[4,128,128]{2,1,0:T(8,128)(2,1)S(1)} collective-permute-done((bf16[4,128,128]{2,1,0:T(8,128)(2,1)S(1)}, bf16[4,128,128]{2,1,0:T(8,128)(2,1)S(1)}, u32[]{:S(2)}, u32[]{:S(2)}) %collective-permute-start.3) | collective-permute-done | bytes 131104 | tf_op jit(solution)/shard_map/ppermute | solution.py:194
  64.0 1.3 collective-permute-done.2
  65.3 2.8 %collective-permute-done.1 = bf16[4,128,128]{2,1,0:T(8,128)(2,1)S(1)} collective-permute-done((bf16[4,128,128]{2,1,0:T(8,128)(2,1)S(1)}, bf16[4,128,128]{2,1,0:T(8,128)(2,1)S(1)}, u32[]{:S(2)}, u32[]{:S(2)}) %collective-permute-start.1) | collective-permute-done | bytes 131104 | tf_op jit(solution)/shard_map/ppermute | solution.py:194
  69.4 1.5 %collective-permute-start.14 = (f32[4,128,128]{2,1,0:T(8,128)S(1)}, f32[4,128,128]{2,1,0:T(8,128)S(1)}, u32[]{:S(2)}, u32[]{:S(2)}) collective-permute-start(f32[4,128,128]{2,1,0:T(8,128)S(1)} %dynamic-slice_add_fusion), channel_id=1, source_target_pairs={{8,0},{12,4},{16,8},{20,12},{24,16},{28,20},{9,1},{13,5},{17,9},{2... | collective-permute-start | bytes 786440 | tf_op jit(solution)/shard_map/ppermute | solution.py:194
  70.9 1.3 collective-permute-start.12
  72.2 1.3 collective-permute-start.13
  73.5 7.7 %shard_map.76 = (bf16[256,8,128]{2,1,0:T(8,128)(2,1)S(1)}, bf16[256,8,128]{2,1,0:T(8,128)(2,1)S(1)}, bf16[256,8,128]{2,1,0:T(8,128)(2,1)S(1)}, bf16[256,32,128]{2,1,0:T(8,128)(2,1)}) custom-call(s32[7]{0:T(128)S(1)} %copy-done.1, bf16[8,1024,128]{2,1,0:T(8,128)(2,1)} %get-tuple-element.25.refs_1_, bf16[8,1024,128]{2,1,0:T(8,128)(2,1)} %get-tuple-element.26.refs_2_.key_ref, ...), custom_call_target="tpu_custom_call" | custom-call | flops 1610612736 | bytes 10485760 | tf_op jit(solution)/shard_map/pallas_call | solution.py:298
  81.2 3.0 %collective-permute-start.5 = (bf16[256,8,128]{2,1,0:T(8,128)(2,1)S(1)}, bf16[256,8,128]{2,1,0:T(8,128)(2,1)S(1)}, u32[]{:S(2)}, u32[]{:S(2)}) collective-permute-start(bf16[256,8,128]{2,1,0:T(8,128)(2,1)S(1)} %get-tuple-element.31), channel_id=1, source_target_pairs={{0,2},{1,3},{2,0},{3,1},{4,6},{5,7},{6,4},{7,5},{8,10},{9,11},{10,... | collective-permute-start | bytes 1572872 | tf_op jit(solution)/shard_map/ppermute | solution.py:317
  86.6 16.5 %shard_map.82 = (bf16[1024,8,128]{2,1,0:T(8,128)(2,1)}, f32[8,1024,128]{2,1,0:T(8,128)S(1)}, f32[8,1024,128]{2,1,0:T(8,128)S(1)}) custom-call(s32[7]{0:T(128)S(1)} %copy-done.1, bf16[8,1024,128]{2,1,0:T(8,128)(2,1)} %get-tuple-element.25.refs_1_, bf16[8,1024,128]{2,1,0:T(8,128)(2,1)} %get-tuple-element.26.refs_2_.key_ref, ...), custom_call_target="tpu_custom_call" | custom-call | flops 3758096384 | bytes 18874368 | tf_op jit(solution)/shard_map/pallas_call | solution.py:353
  103.1 27.2 %collective-permute-done.6.refs_1_ = bf16[256,8,128]{2,1,0:T(8,128)(2,1)S(1)} collective-permute-done((bf16[256,8,128]{2,1,0:T(8,128)(2,1)S(1)}, bf16[256,8,128]{2,1,0:T(8,128)(2,1)S(1)}, u32[]{:S(2)}, u32[]{:S(2)}) %collective-permute-start.6) | collective-permute-done | bytes 524320 | tf_op jit(solution)/shard_map/ppermute | solution.py:317
  130.3 1.5 %shard_map.77.refs_2_ = bf16[256,32,128]{2,1,0:T(8,128)(2,1)} custom-call(s32[7]{0:T(128)S(1)} %copy-done.1, bf16[256,8,128]{2,1,0:T(8,128)(2,1)S(1)} %collective-permute-done.6.refs_1_, bf16[256,8,128]{2,1,0:T(8,128)(2,1)S(1)} %collective-permute-done.7.refs_2_, bf16[256,32,128]{2,1,0:T(8,128)(2,1)} %get-tuple-element.34.refs_3_), custom_call_target="tpu_custom_call", output_to_operand_aliasing={{}: (3, {})} | custom-call | bytes 2097152 | tf_op jit(solution)/shard_map/pallas_call | solution.py:394
  131.9 1.4 shard_map.78
  133.2 6.6 %shard_map.83 = (bf16[1024,8,128]{2,1,0:T(8,128)(2,1)}, bf16[1024,8,128]{2,1,0:T(8,128)(2,1)}) custom-call(s32[7]{0:T(128)S(1)} %copy-done.1, bf16[8,1024,128]{2,1,0:T(8,128)(2,1)} %get-tuple-element.26.refs_2_.key_ref, bf16[8,1024,128]{2,1,0:T(8,128)(2,1)} %get-tuple-element.27.refs_3_.value_ref, f32[8,1024,128]{2,1,0:T(8,128)S(1)} %get-tuple-element.40.key_part, ...), custom_call_target="tpu_custom_call" | custom-call | flops 1073741824 | bytes 16777216 | tf_op jit(solution)/shard_map/pallas_call | solution.py:379
  (27 shorter events, 10.0 us)
Async XLA Ops:
  0.7 5.9 %copy-start = (s32[7]{0:T(128)}, s32[7]{0:T(128)S(1)}, u32[]{:S(2)}) copy-start(s32[7]{0:T(128)S(1)} %stack.28.index_ref.refs_0_) | copy-start | bytes 88
  2.3 24.3 %collective-permute-start.8 = (bf16[256,8,128]{2,1,0:T(8,128)(2,1)S(1)}, bf16[256,8,128]{2,1,0:T(8,128)(2,1)S(1)}, u32[]{:S(2)}, u32[]{:S(2)}) collective-permute-start(bf16[256,8,128]{2,1,0:T(8,128)(2,1)S(1)} %shard_map.80), channel_id=1, source_target_pairs={{0,3},{1,2},{2,1},{3,0},{4,7},{5,6},{6,5},{7,4},{8,11},{9,10},{10,... | collective-permute-start | bytes 1572872 | tf_op jit(solution)/shard_map/ppermute | solution.py:254
  6.7 21.9 %collective-permute-start.9 = (bf16[256,8,128]{2,1,0:T(8,128)(2,1)}, bf16[256,8,128]{2,1,0:T(8,128)(2,1)S(1)}, u32[]{:S(2)}, u32[]{:S(2)}) collective-permute-start(bf16[256,8,128]{2,1,0:T(8,128)(2,1)} %get-tuple-element.36), channel_id=1, source_target_pairs={{0,1},{1,0},{2,3},{3,2},{4,5},{5,4},{6,7},{7,6},{8,9},{9,8},{10,11... | collective-permute-start | bytes 1572872 | tf_op jit(solution)/shard_map/ppermute | solution.py:254
  8.9 39.2 %collective-permute-start.10 = (bf16[256,8,128]{2,1,0:T(8,128)(2,1)}, bf16[256,8,128]{2,1,0:T(8,128)(2,1)S(1)}, u32[]{:S(2)}, u32[]{:S(2)}) collective-permute-start(bf16[256,8,128]{2,1,0:T(8,128)(2,1)} %get-tuple-element.37), channel_id=1, source_target_pairs={{0,2},{1,3},{2,0},{3,1},{4,6},{5,7},{6,4},{7,5},{8,10},{9,11},{10,... | collective-permute-start | bytes 1572872 | tf_op jit(solution)/shard_map/ppermute | solution.py:254
  15.2 32.9 %copy-start.1 = (s32[7]{0:T(128)S(1)}, s32[7]{0:T(128)}, u32[]{:S(2)}) copy-start(s32[7]{0:T(128)} %copy-done) | copy-start | bytes 88
  15.2 40.8 %collective-permute-start = (f32[8,128,128]{2,1,0:T(8,128)}, f32[8,128,128]{2,1,0:T(8,128)S(1)}, u32[]{:S(2)}, u32[]{:S(2)}) collective-permute-start(f32[8,128,128]{2,1,0:T(8,128)} %get-tuple-element.30), channel_id=1, source_target_pairs={{0,4},{4,0},{8,12},{12,8},{16,20},{20,16},{24,28},{28,24},{1,5},{5... | collective-permute-start | bytes 1572872 | tf_op jit(solution)/shard_map/ppermute | solution.py:185
  54.5 14.8 %collective-permute-start.11 = (f32[8,128,128]{2,1,0:T(8,128)S(1)}, f32[8,128,128]{2,1,0:T(8,128)S(1)}, u32[]{:S(2)}, u32[]{:S(2)}) collective-permute-start(f32[8,128,128]{2,1,0:T(8,128)S(1)} %get-tuple-element.43), channel_id=1, source_target_pairs={{0,4},{4,0},{8,12},{12,8},{16,20},{20,16},{24,28},{28,24},{1,5},{5... | collective-permute-start | bytes 1572872 | tf_op jit(solution)/shard_map/ppermute | solution.py:185
  57.0 6.9 %collective-permute-start.3 = (bf16[4,128,128]{2,1,0:T(8,128)(2,1)S(1)}, bf16[4,128,128]{2,1,0:T(8,128)(2,1)S(1)}, u32[]{:S(2)}, u32[]{:S(2)}) collective-permute-start(bf16[4,128,128]{2,1,0:T(8,128)(2,1)S(1)} %fusion), channel_id=1, source_target_pairs={{0,8},{4,12},{8,16},{12,20},{16,24},{20,28},{1,9},{5,13},{9,17},{1... | collective-permute-start | bytes 393224 | tf_op jit(solution)/shard_map/ppermute | solution.py:194
  58.3 6.9 %collective-permute-start.2 = (bf16[4,128,128]{2,1,0:T(8,128)(2,1)S(1)}, bf16[4,128,128]{2,1,0:T(8,128)(2,1)S(1)}, u32[]{:S(2)}, u32[]{:S(2)}) collective-permute-start(bf16[4,128,128]{2,1,0:T(8,128)(2,1)S(1)} %fusion), channel_id=1, source_target_pairs={{0,16},{4,20},{8,24},{12,28},{1,17},{5,21},{9,25},{13,29},{2,18},{... | collective-permute-start | bytes 393224 | tf_op jit(solution)/shard_map/ppermute | solution.py:194
  59.6 8.5 %collective-permute-start.1 = (bf16[4,128,128]{2,1,0:T(8,128)(2,1)S(1)}, bf16[4,128,128]{2,1,0:T(8,128)(2,1)S(1)}, u32[]{:S(2)}, u32[]{:S(2)}) collective-permute-start(bf16[4,128,128]{2,1,0:T(8,128)(2,1)S(1)} %fusion), channel_id=1, source_target_pairs={{0,24},{4,28},{1,25},{5,29},{2,26},{6,30},{3,27},{7,31}} | collective-permute-start | bytes 393224 | tf_op jit(solution)/shard_map/ppermute | solution.py:194
  68.1 5.4 %collective-permute-start.4 = (f32[4,128,128]{2,1,0:T(8,128)S(1)}, f32[4,128,128]{2,1,0:T(8,128)S(1)}, u32[]{:S(2)}, u32[]{:S(2)}) collective-permute-start(f32[4,128,128]{2,1,0:T(8,128)S(1)} %convert_add_fusion.refs_7_), channel_id=1, source_target_pairs={{0,4},{4,0},{8,12},{12,8},{16,20},{20,16},{24,28},{28,24},{1,5},{5... | collective-permute-start | bytes 786440 | tf_op jit(solution)/shard_map/ppermute | solution.py:195
  69.4 15.0 %collective-permute-start.14 = (f32[4,128,128]{2,1,0:T(8,128)S(1)}, f32[4,128,128]{2,1,0:T(8,128)S(1)}, u32[]{:S(2)}, u32[]{:S(2)}) collective-permute-start(f32[4,128,128]{2,1,0:T(8,128)S(1)} %dynamic-slice_add_fusion), channel_id=1, source_target_pairs={{8,0},{12,4},{16,8},{20,12},{24,16},{28,20},{9,1},{13,5},{17,9},{2... | collective-permute-start | bytes 786440 | tf_op jit(solution)/shard_map/ppermute | solution.py:194
  70.9 14.5 %collective-permute-start.12 = (f32[4,128,128]{2,1,0:T(8,128)S(1)}, f32[4,128,128]{2,1,0:T(8,128)S(1)}, u32[]{:S(2)}, u32[]{:S(2)}) collective-permute-start(f32[4,128,128]{2,1,0:T(8,128)S(1)} %dynamic-slice_add_fusion), channel_id=1, source_target_pairs={{24,0},{28,4},{25,1},{29,5},{26,2},{30,6},{27,3},{31,7}} | collective-permute-start | bytes 786440 | tf_op jit(solution)/shard_map/ppermute | solution.py:194
  72.2 13.2 %collective-permute-start.13 = (f32[4,128,128]{2,1,0:T(8,128)S(1)}, f32[4,128,128]{2,1,0:T(8,128)S(1)}, u32[]{:S(2)}, u32[]{:S(2)}) collective-permute-start(f32[4,128,128]{2,1,0:T(8,128)S(1)} %dynamic-slice_add_fusion), channel_id=1, source_target_pairs={{16,0},{20,4},{24,8},{28,12},{17,1},{21,5},{25,9},{29,13},{18,2},{... | collective-permute-start | bytes 786440 | tf_op jit(solution)/shard_map/ppermute | solution.py:194
  81.2 50.7 %collective-permute-start.5 = (bf16[256,8,128]{2,1,0:T(8,128)(2,1)S(1)}, bf16[256,8,128]{2,1,0:T(8,128)(2,1)S(1)}, u32[]{:S(2)}, u32[]{:S(2)}) collective-permute-start(bf16[256,8,128]{2,1,0:T(8,128)(2,1)S(1)} %get-tuple-element.31), channel_id=1, source_target_pairs={{0,2},{1,3},{2,0},{3,1},{4,6},{5,7},{6,4},{7,5},{8,10},{9,11},{10,... | collective-permute-start | bytes 1572872 | tf_op jit(solution)/shard_map/ppermute | solution.py:317
  84.2 46.1 %collective-permute-start.6 = (bf16[256,8,128]{2,1,0:T(8,128)(2,1)S(1)}, bf16[256,8,128]{2,1,0:T(8,128)(2,1)S(1)}, u32[]{:S(2)}, u32[]{:S(2)}) collective-permute-start(bf16[256,8,128]{2,1,0:T(8,128)(2,1)S(1)} %get-tuple-element.32), channel_id=1, source_target_pairs={{0,3},{1,2},{2,1},{3,0},{4,7},{5,6},{6,5},{7,4},{8,11},{9,10},{10,... | collective-permute-start | bytes 1572872 | tf_op jit(solution)/shard_map/ppermute | solution.py:317
  84.4 46.0 %collective-permute-start.7 = (bf16[256,8,128]{2,1,0:T(8,128)(2,1)S(1)}, bf16[256,8,128]{2,1,0:T(8,128)(2,1)S(1)}, u32[]{:S(2)}, u32[]{:S(2)}) collective-permute-start(bf16[256,8,128]{2,1,0:T(8,128)(2,1)S(1)} %get-tuple-element.33), channel_id=1, source_target_pairs={{0,1},{1,0},{2,3},{3,2},{4,5},{5,4},{6,7},{7,6},{8,9},{9,8},{10,11... | collective-permute-start | bytes 1572872 | tf_op jit(solution)/shard_map/ppermute | solution.py:317
  85.4 47.8 %collective-permute-start.15 = (f32[4,128,128]{2,1,0:T(8,128)S(1)}, f32[4,128,128]{2,1,0:T(8,128)S(1)}, u32[]{:S(2)}, u32[]{:S(2)}) collective-permute-start(f32[4,128,128]{2,1,0:T(8,128)S(1)} %add_add_fusion.refs_1_), channel_id=1, source_target_pairs={{0,4},{4,0},{8,12},{12,8},{16,20},{20,16},{24,28},{28,24},{1,5},{5... | collective-permute-start | bytes 786440 | tf_op jit(solution)/shard_map/ppermute | solution.py:195

commit v4 on v3

--- a/solution.py
+++ b/solution.py
@@ -103,28 +103,26 @@
 
 def local_grad_kernel(index_ref, query_ref, key_ref, value_ref, grad_ref, before_ref, *refs):
     prefix_refs = refs[:3]
-    query_out, key_out, value_out, held, base = refs[3:]
-    j = pl.program_id(1)
-    half, rows = query_ref.shape[:2]
+    query_out, key_out, value_out, held, base, scores, scores_t, within_t = refs[3:]
+    heads, rows = query_ref.shape[:2]
     lower = iota(rows, 1) <= iota(rows, 0)
     upper = iota(rows, 0) <= iota(rows, 1)
 
     @pl.when(pl.program_id(0) == 0)
     def _():
-        for h in range(half):
-            base[j * half + h] = base_state(prefix_refs, index_ref[1], j, False, half, h)
-
-    for h in range(half):
-        query, key, value, grad = query_ref[h], key_ref[h], value_ref[h], grad_ref[h]
-        state = (base[j * half + h] + before_ref[h, 0]).astype(BF16)
-        scores = masked(lower, dot(grad, value, 1, 1))
-        held[j * half + h] = (dot(grad, state, 1, 1) + dot(scores, key, 1, 0)).astype(BF16)
-        key_out[h] = dot(masked(upper, dot(value, grad, 1, 1)), query, 1, 0)
-        value_out[h] = dot(masked(upper, dot(key, query, 1, 1)), grad, 1, 0)
-
-    @pl.when(j == 1)
-    def _():
-        query_out[...] = jnp.swapaxes(held[...], 0, 1)
+        for h in range(heads):
+            base[h] = base_state(prefix_refs, index_ref[1], h // (heads // 2), False, heads // 2, h % (heads // 2))
+
+    for h in range(heads):
+        scores[h] = masked(lower, dot(grad_ref[h], value_ref[h], 1, 1))
+        scores_t[h] = masked(upper, dot(value_ref[h], grad_ref[h], 1, 1))
+        within_t[h] = masked(upper, dot(key_ref[h], query_ref[h], 1, 1))
+    for h in range(heads):
+        state = (base[h] + before_ref[h, 0]).astype(BF16)
+        held[h] = (dot(grad_ref[h], state, 1, 1) + dot(scores[h], key_ref[h], 1, 0)).astype(BF16)
+        key_out[h] = dot(scores_t[h], query_ref[h], 1, 0)
+        value_out[h] = dot(within_t[h], grad_ref[h], 1, 0)
+    query_out[...] = jnp.swapaxes(held[...], 0, 1)
 
 
 def later_grad_kernel(index_ref, key_ref, value_ref, key_part, value_part, state_ref, *refs):
@@ -184,8 +182,7 @@
     swap = [(i, i ^ 1) for i in range(n_seq)]
     twin = lax.ppermute(total, "seq", swap)
     mine = lax.dynamic_slice_in_dim(total + twin, core * half, half, 0)
-    if not later:
-        mine = mine.astype(BF16)
+    mine = mine.astype(BF16)
     acc = jnp.zeros(mine.shape, F32)
     for step in range(n_seq // 2 - 1, 0, -1):
         hops = [(i, i + 2 * step) for i in range(n_seq - 2 * step)]
@@ -249,7 +246,8 @@
 
     pieces = {}
     picked = dict(zip(order[:1], pick(order[:1])))
-    picked.update(zip(order[1:] + [0], pick(order[1:] + [0])))
+    picked.update(zip(order[1:], pick(order[1:])))
+    picked[0] = pick([0])[0]
     for r in order:
         pieces[r] = lax.ppermute(picked[r], "head", [(i, i ^ r) for i in range(n_head)])
     pieces[0] = picked[0]
@@ -341,7 +339,7 @@
             {4 + count: 0, 5 + count: 1} if extra else {},
         )(place, *hbm(query, scale), *[pieces[r] for r in proc[first : first + count]], *extra)
 
-    early = n_head
+    early = max(n_head - 1, 1)
     grad, states, total = grad_state("grad_state_early", early, 0, ())
     early_grad = grad
     if early < n_head:
@@ -349,21 +347,22 @@
     suffix = other_segments(total, True, n_seq)
 
     def local_grad(name, count, first, grad, outs):
-        chunk_rows = pl.BlockSpec((half, chunk, size), lambda c, j, i: (j, i[3 + first + c], 0))
+        chunk_rows = pl.BlockSpec((heads, chunk, size), lambda c, i: (0, i[3 + first + c], 0))
         return call(
             lambda *refs: local_grad_kernel(*refs[:9], *refs[9 + len(outs) :]),
-            (count, 2),
+            (count,),
             [chunk_rows] * 4
-            + [pl.BlockSpec((half, 1, size, size), lambda c, j, i: (j, i[3 + first + c], 0, 0))]
+            + [pl.BlockSpec((heads, 1, size, size), lambda c, i: (0, i[3 + first + c], 0, 0))]
             + other_specs
             + [any_spec] * len(outs),
-            [pl.BlockSpec((chunk, heads, size), lambda c, j, i: (i[3 + first + c], 0, 0)), chunk_rows, chunk_rows],
+            [pl.BlockSpec((chunk, heads, size), lambda c, i: (i[3 + first + c], 0, 0)), chunk_rows, chunk_rows],
             [
                 array((tok_rows, heads, size), BF16),
                 array((heads, tok_rows, size), F32),
                 array((heads, tok_rows, size), F32),
             ],
-            [pltpu.VMEM((heads, chunk, size), BF16), pltpu.VMEM((heads, size, size), F32)],
+            [pltpu.VMEM((heads, chunk, size), BF16), pltpu.VMEM((heads, size, size), F32)]
+            + [pltpu.VMEM((heads, chunk, chunk), BF16)] * 3,
             cost(7 * unit * count // n_chunk, 9 * full_bytes * count // n_chunk),
             name,
             {9 + k: k for k in range(len(outs))},

time: 141 us -> 150 us (1.064)
  the two profiles are of different devices: /device:TPU:15 before, /device:TPU:0 now
where the time goes in v4:
time: 150 us; the launch traced here: 149 us
  waiting for transfers between devices  62.4 us (42%)
  Pallas kernels  57.9 us (39%)
  starting transfers between devices  26.3 us (18%)
    ppermute x3, waiting for transfers between devices, per_device(): lax.ppermute(parts[proc.index(r) - 1], 'head', [(i, i ^ r) for i in range...  35 us
    ppermute x3, waiting for transfers between devices, per_device(): lax.ppermute(picked[r], 'head', [(i, i ^ r) for i in range(n_head)])  23.7 us
    pallas_call x2, Pallas kernels, local_grad(): call(lambda *refs: local_grad_kernel(*refs[:9], *refs[9 + len(outs):]), (...  14.3 us
    ppermute x6, starting transfers between devices, other_segments(): acc = acc + lax.ppermute(mine, 'seq', hops).astype(F32)  13.4 us
    pallas_call x2, Pallas kernels, grad_state(): call(lambda *refs: grad_state_kernel(count, *refs[:3 + count], *refs[3 +...  8.73 us
    ppermute x3, starting transfers between devices, per_device(): lax.ppermute(parts[proc.index(r) - 1], 'head', [(i, i ^ r) for i in range...  7.88 us
    pallas_call x1, Pallas kernels, per_device(): call(lambda *refs: attended_kernel(n_head, *refs), (n_head,), [rows_spec]...  7.64 us
    pallas_call x3, Pallas kernels, pick(): call(lambda *refs: pick_kernel(steps, heads, *refs), (1,), [any_spec], [i...  6.73 us
  transfers between devices with their start and end apart: 16, of which 8 were waited for; matrix products, arithmetic and copies ran while one was open for 0% of the time, Pallas kernels for 28%

profile of v4, /device:TPU:0, one launch (start us, length us, event | category | flops | bytes accessed | tf_op | source)
XLA Modules:
  0.0 148.6 jit_solution(748836616317685933)
XLA Ops:
  0.6 6.3 %key_state.1 = (bf16[8,1024,128]{2,1,0:T(8,128)(2,1)}, bf16[8,1024,128]{2,1,0:T(8,128)(2,1)}, f32[8,4,128,128]{3,2,1,0:T(8,128)}, f32[8,128,128]{2,1,0:T(8,128)}) custom-call(bf16[1024,8,128]{2,1,0:T(8,128)(2,1)} %key_ref.1, bf16[1024,8,128]{2,1,0:T(8,128)(2,1)} %value_ref.1), custom_call_target="tpu_custom_call" | custom-call | flops 536870912 | bytes 10485760 | tf_op jit(solution)/shard_map/key_state/pallas_call | solution.py:265
  7.5 1.7 %collective-permute-done.refs_6_ = f32[8,128,128]{2,1,0:T(8,128)S(1)} collective-permute-done((f32[8,128,128]{2,1,0:T(8,128)}, f32[8,128,128]{2,1,0:T(8,128)S(1)}, u32[]{:S(2)}, u32[]{:S(2)}) %collective-permute-start) | collective-permute-done | bytes 524320 | tf_op jit(solution)/shard_map/ppermute | solution.py:183
  10.2 5.7 %collective-permute-start.1 = (bf16[4,128,128]{2,1,0:T(8,128)(2,1)S(1)}, bf16[4,128,128]{2,1,0:T(8,128)(2,1)S(1)}, u32[]{:S(2)}, u32[]{:S(2)}) collective-permute-start(bf16[4,128,128]{2,1,0:T(8,128)(2,1)S(1)} %fusion.1), channel_id=1, source_target_pairs={{0,24},{4,28},{1,25},{5,29},{2,26},{6,30},{3,27},{7,31}} | collective-permute-start | bytes 393224 | tf_op jit(solution)/shard_map/ppermute | solution.py:191
  17.2 2.5 %collective-permute-start.3 = (bf16[4,128,128]{2,1,0:T(8,128)(2,1)S(1)}, bf16[4,128,128]{2,1,0:T(8,128)(2,1)S(1)}, u32[]{:S(2)}, u32[]{:S(2)}) collective-permute-start(bf16[4,128,128]{2,1,0:T(8,128)(2,1)S(1)} %fusion.1), channel_id=1, source_target_pairs={{0,8},{4,12},{8,16},{12,20},{16,24},{20,28},{1,9},{5,13},{9,17},{1... | collective-permute-start | bytes 393224 | tf_op jit(solution)/shard_map/ppermute | solution.py:191
  19.8 2.7 %shard_map.79 = (bf16[256,8,128]{2,1,0:T(8,128)(2,1)}, bf16[256,8,128]{2,1,0:T(8,128)(2,1)}) custom-call(s32[7]{0:T(128)S(1)} %stack.28.index_ref.refs_0_, bf16[256,32,128]{2,1,0:T(8,128)(2,1)} %refs_1_.5), custom_call_target="tpu_custom_call" | custom-call | bytes 2097152 | tf_op jit(solution)/shard_map/pallas_call | solution.py:236
  22.5 1.6 %collective-permute-start.10 = (bf16[256,8,128]{2,1,0:T(8,128)(2,1)}, bf16[256,8,128]{2,1,0:T(8,128)(2,1)S(1)}, u32[]{:S(2)}, u32[]{:S(2)}) collective-permute-start(bf16[256,8,128]{2,1,0:T(8,128)(2,1)} %get-tuple-element.41), channel_id=1, source_target_pairs={{0,1},{1,0},{2,3},{3,2},{4,5},{5,4},{6,7},{7,6},{8,9},{9,8},{10,11... | collective-permute-start | bytes 1572872 | tf_op jit(solution)/shard_map/ppermute | solution.py:252
  24.2 2.4 %shard_map.81 = bf16[256,8,128]{2,1,0:T(8,128)(2,1)} custom-call(s32[7]{0:T(128)S(1)} %stack.28.index_ref.refs_0_, bf16[256,32,128]{2,1,0:T(8,128)(2,1)} %refs_1_.5), custom_call_target="tpu_custom_call" | custom-call | bytes 1048576 | tf_op jit(solution)/shard_map/pallas_call | solution.py:236
  26.6 2.5 %collective-permute-start.9 = (bf16[256,8,128]{2,1,0:T(8,128)(2,1)}, bf16[256,8,128]{2,1,0:T(8,128)(2,1)S(1)}, u32[]{:S(2)}, u32[]{:S(2)}) collective-permute-start(bf16[256,8,128]{2,1,0:T(8,128)(2,1)} %shard_map.81), channel_id=1, source_target_pairs={{0,3},{1,2},{2,1},{3,0},{4,7},{5,6},{6,5},{7,4},{8,11},{9,10},{10,... | collective-permute-start | bytes 1572872 | tf_op jit(solution)/shard_map/ppermute | solution.py:252
  29.5 1.6 %shard_map.80.refs_3_ = bf16[256,8,128]{2,1,0:T(8,128)(2,1)S(1)} custom-call(s32[7]{0:T(128)S(1)} %stack.28.index_ref.refs_0_, bf16[256,32,128]{2,1,0:T(8,128)(2,1)} %refs_1_.5), custom_call_target="tpu_custom_call" | custom-call | bytes 1048576 | tf_op jit(solution)/shard_map/pallas_call | solution.py:236
  31.1 4.8 %shard_map.75 = (bf16[8,1024,128]{2,1,0:T(8,128)(2,1)}, f32[1024,128]{1,0:T(8,128)}) custom-call(s32[7]{0:T(128)} %copy-done, bf16[1024,8,128]{2,1,0:T(8,128)(2,1)} %query_ref.1), custom_call_target="tpu_custom_call" | custom-call | flops 134217728 | bytes 4194304 | tf_op jit(solution)/shard_map/pallas_call | solution.py:280
  36.8 14.2 %collective-permute-done.9.refs_4_ = bf16[256,8,128]{2,1,0:T(8,128)(2,1)S(1)} collective-permute-done((bf16[256,8,128]{2,1,0:T(8,128)(2,1)}, bf16[256,8,128]{2,1,0:T(8,128)(2,1)S(1)}, u32[]{:S(2)}, u32[]{:S(2)}) %collective-permute-start.9) | collective-permute-done | bytes 524320 | tf_op jit(solution)/shard_map/ppermute | solution.py:252
  51.0 5.5 %shard_map.82 = (bf16[8,1024,128]{2,1,0:T(8,128)(2,1)}, f32[4,8,128,128]{3,2,1,0:T(8,128)}, f32[8,128,128]{2,1,0:T(8,128)S(1)}) custom-call(s32[7]{0:T(128)S(1)} %copy-done.1, bf16[8,1024,128]{2,1,0:T(8,128)(2,1)} %get-tuple-element.30.refs_1_, f32[1024,128]{1,0:T(8,128)} %get-tuple-element.34.refs_5_.refs_2_, bf16[256,8,128]{2,1,0:T(8,128)(2,1)S(1)} %shard_map.80.refs_3_, ...), custom_call_target="tpu_custom_call" | custom-call | flops 402653184 | bytes 6291456 | tf_op jit(solution)/shard_map/pallas_call | solution.py:321
  56.5 9.4 %shard_map.84 = (bf16[1024,8,128]{2,1,0:T(8,128)(2,1)}, f32[8,1024,128]{2,1,0:T(8,128)S(1)}, f32[8,1024,128]{2,1,0:T(8,128)S(1)}) custom-call(s32[7]{0:T(128)S(1)} %copy-done.1, bf16[8,1024,128]{2,1,0:T(8,128)(2,1)} %get-tuple-element.30.refs_1_, bf16[8,1024,128]{2,1,0:T(8,128)(2,1)} %get-tuple-element.31.refs_2_.key_ref, ...), custom_call_target="tpu_custom_call" | custom-call | flops 2818572288 | bytes 14155776 | tf_op jit(solution)/shard_map/pallas_call | solution.py:351
  66.0 8.6 %collective-permute-done.8.refs_3_ = bf16[256,8,128]{2,1,0:T(8,128)(2,1)S(1)} collective-permute-done((bf16[256,8,128]{2,1,0:T(8,128)(2,1)}, bf16[256,8,128]{2,1,0:T(8,128)(2,1)S(1)}, u32[]{:S(2)}, u32[]{:S(2)}) %collective-permute-start.8) | collective-permute-done | bytes 524320 | tf_op jit(solution)/shard_map/ppermute | solution.py:252
  74.5 3.2 %shard_map.83 = (bf16[8,1024,128]{2,1,0:T(8,128)(2,1)}, f32[4,8,128,128]{3,2,1,0:T(8,128)}, f32[8,128,128]{2,1,0:T(8,128)S(1)}) custom-call(s32[7]{0:T(128)S(1)} %copy-done.1, bf16[8,1024,128]{2,1,0:T(8,128)(2,1)} %get-tuple-element.30.refs_1_, f32[1024,128]{1,0:T(8,128)} %get-tuple-element.34.refs_5_.refs_2_, ...), custom_call_target="tpu_custom_call", output_to_operand_aliasing={{0}: (5, {}), {1}: (6, {})} | custom-call | flops 134217728 | bytes 2097152 | tf_op jit(solution)/shard_map/pallas_call | solution.py:321
  77.7 1.9 %collective-permute-done.11.refs_0_ = f32[8,128,128]{2,1,0:T(8,128)S(1)} collective-permute-done((f32[8,128,128]{2,1,0:T(8,128)S(1)}, f32[8,128,128]{2,1,0:T(8,128)S(1)}, u32[]{:S(2)}, u32[]{:S(2)}) %collective-permute-start.11) | collective-permute-done | bytes 524320 | tf_op jit(solution)/shard_map/ppermute | solution.py:183
  83.6 7.6 %shard_map.76 = (bf16[256,8,128]{2,1,0:T(8,128)(2,1)S(1)}, bf16[256,8,128]{2,1,0:T(8,128)(2,1)S(1)}, bf16[256,8,128]{2,1,0:T(8,128)(2,1)S(1)}, bf16[256,32,128]{2,1,0:T(8,128)(2,1)}) custom-call(s32[7]{0:T(128)S(1)} %copy-done.1, bf16[8,1024,128]{2,1,0:T(8,128)(2,1)} %get-tuple-element.30.refs_1_, bf16[8,1024,128]{2,1,0:T(8,128)(2,1)} %get-tuple-element.31.refs_2_.key_ref, ...), custom_call_target="tpu_custom_call" | custom-call | flops 1610612736 | bytes 10485760 | tf_op jit(solution)/shard_map/pallas_call | solution.py:296
  91.2 2.6 %collective-permute-start.6 = (bf16[256,8,128]{2,1,0:T(8,128)(2,1)S(1)}, bf16[256,8,128]{2,1,0:T(8,128)(2,1)S(1)}, u32[]{:S(2)}, u32[]{:S(2)}) collective-permute-start(bf16[256,8,128]{2,1,0:T(8,128)(2,1)S(1)} %get-tuple-element.37), channel_id=1, source_target_pairs={{0,3},{1,2},{2,1},{3,0},{4,7},{5,6},{6,5},{7,4},{8,11},{9,10},{10,... | collective-permute-start | bytes 1572872 | tf_op jit(solution)/shard_map/ppermute | solution.py:315
  93.8 5.2 %collective-permute-start.7 = (bf16[256,8,128]{2,1,0:T(8,128)(2,1)S(1)}, bf16[256,8,128]{2,1,0:T(8,128)(2,1)S(1)}, u32[]{:S(2)}, u32[]{:S(2)}) collective-permute-start(bf16[256,8,128]{2,1,0:T(8,128)(2,1)S(1)} %get-tuple-element.38), channel_id=1, source_target_pairs={{0,1},{1,0},{2,3},{3,2},{4,5},{5,4},{6,7},{7,6},{8,9},{9,8},{10,11... | collective-permute-start | bytes 1572872 | tf_op jit(solution)/shard_map/ppermute | solution.py:315
  99.3 4.9 %shard_map.85 = (bf16[1024,8,128]{2,1,0:T(8,128)(2,1)}, f32[8,1024,128]{2,1,0:T(8,128)S(1)}, f32[8,1024,128]{2,1,0:T(8,128)S(1)}) custom-call(s32[7]{0:T(128)S(1)} %copy-done.1, bf16[8,1024,128]{2,1,0:T(8,128)(2,1)} %get-tuple-element.30.refs_1_, ...), custom_call_target="tpu_custom_call", output_to_operand_aliasing={{0}: (9, {}), {1}: (10, {}), {2}: (11, {})} | custom-call | flops 939524096 | bytes 4718592 | tf_op jit(solution)/shard_map/pallas_call | solution.py:351
  104.2 3.7 %collective-permute-done.6.refs_1_ = bf16[256,8,128]{2,1,0:T(8,128)(2,1)S(1)} collective-permute-done((bf16[256,8,128]{2,1,0:T(8,128)(2,1)S(1)}, bf16[256,8,128]{2,1,0:T(8,128)(2,1)S(1)}, u32[]{:S(2)}, u32[]{:S(2)}) %collective-permute-start.6) | collective-permute-done | bytes 524320 | tf_op jit(solution)/shard_map/ppermute | solution.py:315
  107.9 10.4 %collective-permute-done.7.refs_2_ = bf16[256,8,128]{2,1,0:T(8,128)(2,1)S(1)} collective-permute-done((bf16[256,8,128]{2,1,0:T(8,128)(2,1)S(1)}, bf16[256,8,128]{2,1,0:T(8,128)(2,1)S(1)}, u32[]{:S(2)}, u32[]{:S(2)}) %collective-permute-start.7) | collective-permute-done | bytes 524320 | tf_op jit(solution)/shard_map/ppermute | solution.py:315
  119.8 20.9 %collective-permute-done.5.refs_1_ = bf16[256,8,128]{2,1,0:T(8,128)(2,1)S(1)} collective-permute-done((bf16[256,8,128]{2,1,0:T(8,128)(2,1)S(1)}, bf16[256,8,128]{2,1,0:T(8,128)(2,1)S(1)}, u32[]{:S(2)}, u32[]{:S(2)}) %collective-permute-start.5) | collective-permute-done | bytes 524320 | tf_op jit(solution)/shard_map/ppermute | solution.py:315
  142.1 6.6 %shard_map.86 = (bf16[1024,8,128]{2,1,0:T(8,128)(2,1)}, bf16[1024,8,128]{2,1,0:T(8,128)(2,1)}) custom-call(s32[7]{0:T(128)S(1)} %copy-done.1, bf16[8,1024,128]{2,1,0:T(8,128)(2,1)} %get-tuple-element.31.refs_2_.key_ref, bf16[8,1024,128]{2,1,0:T(8,128)(2,1)} %get-tuple-element.32.refs_3_.value_ref, f32[8,1024,128]{2,1,0:T(8,128)S(1)} %get-tuple-element.50.key_part, ...), custom_call_target="tpu_custom_call" | custom-call | flops 1073741824 | bytes 16777216 | tf_op jit(solution)/shard_map/pallas_call | solution.py:378
  (30 shorter events, 11.1 us)
Async XLA Ops:
  6.9 2.3 %collective-permute-start = (f32[8,128,128]{2,1,0:T(8,128)}, f32[8,128,128]{2,1,0:T(8,128)S(1)}, u32[]{:S(2)}, u32[]{:S(2)}) collective-permute-start(f32[8,128,128]{2,1,0:T(8,128)} %get-tuple-element.35), channel_id=1, source_target_pairs={{0,4},{4,0},{8,12},{12,8},{16,20},{20,16},{24,28},{28,24},{1,5},{5... | collective-permute-start | bytes 1572872 | tf_op jit(solution)/shard_map/ppermute | solution.py:183
  10.2 18.9 %collective-permute-start.1 = (bf16[4,128,128]{2,1,0:T(8,128)(2,1)S(1)}, bf16[4,128,128]{2,1,0:T(8,128)(2,1)S(1)}, u32[]{:S(2)}, u32[]{:S(2)}) collective-permute-start(bf16[4,128,128]{2,1,0:T(8,128)(2,1)S(1)} %fusion.1), channel_id=1, source_target_pairs={{0,24},{4,28},{1,25},{5,29},{2,26},{6,30},{3,27},{7,31}} | collective-permute-start | bytes 393224 | tf_op jit(solution)/shard_map/ppermute | solution.py:191
  15.9 13.2 %collective-permute-start.2 = (bf16[4,128,128]{2,1,0:T(8,128)(2,1)S(1)}, bf16[4,128,128]{2,1,0:T(8,128)(2,1)S(1)}, u32[]{:S(2)}, u32[]{:S(2)}) collective-permute-start(bf16[4,128,128]{2,1,0:T(8,128)(2,1)S(1)} %fusion.1), channel_id=1, source_target_pairs={{0,16},{4,20},{8,24},{12,28},{1,17},{5,21},{9,25},{13,29},{2,18},{... | collective-permute-start | bytes 393224 | tf_op jit(solution)/shard_map/ppermute | solution.py:191
  17.2 11.9 %collective-permute-start.3 = (bf16[4,128,128]{2,1,0:T(8,128)(2,1)S(1)}, bf16[4,128,128]{2,1,0:T(8,128)(2,1)S(1)}, u32[]{:S(2)}, u32[]{:S(2)}) collective-permute-start(bf16[4,128,128]{2,1,0:T(8,128)(2,1)S(1)} %fusion.1), channel_id=1, source_target_pairs={{0,8},{4,12},{8,16},{12,20},{16,24},{20,28},{1,9},{5,13},{9,17},{1... | collective-permute-start | bytes 393224 | tf_op jit(solution)/shard_map/ppermute | solution.py:191
  19.8 9.7 %copy-start = (s32[7]{0:T(128)}, s32[7]{0:T(128)S(1)}, u32[]{:S(2)}) copy-start(s32[7]{0:T(128)S(1)} %stack.28.index_ref.refs_0_) | copy-start | bytes 88
  22.5 14.3 %collective-permute-start.10 = (bf16[256,8,128]{2,1,0:T(8,128)(2,1)}, bf16[256,8,128]{2,1,0:T(8,128)(2,1)S(1)}, u32[]{:S(2)}, u32[]{:S(2)}) collective-permute-start(bf16[256,8,128]{2,1,0:T(8,128)(2,1)} %get-tuple-element.41), channel_id=1, source_target_pairs={{0,1},{1,0},{2,3},{3,2},{4,5},{5,4},{6,7},{7,6},{8,9},{9,8},{10,11... | collective-permute-start | bytes 1572872 | tf_op jit(solution)/shard_map/ppermute | solution.py:252
  26.6 24.4 %collective-permute-start.9 = (bf16[256,8,128]{2,1,0:T(8,128)(2,1)}, bf16[256,8,128]{2,1,0:T(8,128)(2,1)S(1)}, u32[]{:S(2)}, u32[]{:S(2)}) collective-permute-start(bf16[256,8,128]{2,1,0:T(8,128)(2,1)} %shard_map.81), channel_id=1, source_target_pairs={{0,3},{1,2},{2,1},{3,0},{4,7},{5,6},{6,5},{7,4},{8,11},{9,10},{10,... | collective-permute-start | bytes 1572872 | tf_op jit(solution)/shard_map/ppermute | solution.py:252
  29.2 27.3 %collective-permute-start.4 = (f32[4,128,128]{2,1,0:T(8,128)S(1)}, f32[4,128,128]{2,1,0:T(8,128)S(1)}, u32[]{:S(2)}, u32[]{:S(2)}) collective-permute-start(f32[4,128,128]{2,1,0:T(8,128)S(1)} %convert_add_fusion.1.refs_7_), channel_id=1, source_target_pairs={{0,4},{4,0},{8,12},{12,8},{16,20},{20,16},{24,28},{28,24},{1,5},{5... | collective-permute-start | bytes 786440 | tf_op jit(solution)/shard_map/ppermute | solution.py:192
  29.3 45.3 %collective-permute-start.8 = (bf16[256,8,128]{2,1,0:T(8,128)(2,1)}, bf16[256,8,128]{2,1,0:T(8,128)(2,1)S(1)}, u32[]{:S(2)}, u32[]{:S(2)}) collective-permute-start(bf16[256,8,128]{2,1,0:T(8,128)(2,1)} %get-tuple-element.40), channel_id=1, source_target_pairs={{0,2},{1,3},{2,0},{3,1},{4,6},{5,7},{6,4},{7,5},{8,10},{9,11},{10,... | collective-permute-start | bytes 1572872 | tf_op jit(solution)/shard_map/ppermute | solution.py:252
  31.1 19.9 %copy-start.1 = (s32[7]{0:T(128)S(1)}, s32[7]{0:T(128)}, u32[]{:S(2)}) copy-start(s32[7]{0:T(128)} %copy-done) | copy-start | bytes 88
  77.7 1.9 %collective-permute-start.11 = (f32[8,128,128]{2,1,0:T(8,128)S(1)}, f32[8,128,128]{2,1,0:T(8,128)S(1)}, u32[]{:S(2)}, u32[]{:S(2)}) collective-permute-start(f32[8,128,128]{2,1,0:T(8,128)S(1)} %get-tuple-element.53), channel_id=1, source_target_pairs={{0,4},{4,0},{8,12},{12,8},{16,20},{20,16},{24,28},{28,24},{1,5},{5... | collective-permute-start | bytes 1572872 | tf_op jit(solution)/shard_map/ppermute | solution.py:183
  79.7 19.4 %collective-permute-start.12 = (bf16[4,128,128]{2,1,0:T(8,128)(2,1)S(1)}, bf16[4,128,128]{2,1,0:T(8,128)(2,1)S(1)}, u32[]{:S(2)}, u32[]{:S(2)}) collective-permute-start(bf16[4,128,128]{2,1,0:T(8,128)(2,1)S(1)} %fusion), channel_id=1, source_target_pairs={{24,0},{28,4},{25,1},{29,5},{26,2},{30,6},{27,3},{31,7}} | collective-permute-start | bytes 393224 | tf_op jit(solution)/shard_map/ppermute | solution.py:191
  81.0 18.1 %collective-permute-start.13 = (bf16[4,128,128]{2,1,0:T(8,128)(2,1)S(1)}, bf16[4,128,128]{2,1,0:T(8,128)(2,1)S(1)}, u32[]{:S(2)}, u32[]{:S(2)}) collective-permute-start(bf16[4,128,128]{2,1,0:T(8,128)(2,1)S(1)} %fusion), channel_id=1, source_target_pairs={{16,0},{20,4},{24,8},{28,12},{17,1},{21,5},{25,9},{29,13},{18,2},{... | collective-permute-start | bytes 393224 | tf_op jit(solution)/shard_map/ppermute | solution.py:191
  82.3 16.8 %collective-permute-start.14 = (bf16[4,128,128]{2,1,0:T(8,128)(2,1)S(1)}, bf16[4,128,128]{2,1,0:T(8,128)(2,1)S(1)}, u32[]{:S(2)}, u32[]{:S(2)}) collective-permute-start(bf16[4,128,128]{2,1,0:T(8,128)(2,1)S(1)} %fusion), channel_id=1, source_target_pairs={{8,0},{12,4},{16,8},{20,12},{24,16},{28,20},{9,1},{13,5},{17,9},{2... | collective-permute-start | bytes 393224 | tf_op jit(solution)/shard_map/ppermute | solution.py:191
  91.2 16.6 %collective-permute-start.6 = (bf16[256,8,128]{2,1,0:T(8,128)(2,1)S(1)}, bf16[256,8,128]{2,1,0:T(8,128)(2,1)S(1)}, u32[]{:S(2)}, u32[]{:S(2)}) collective-permute-start(bf16[256,8,128]{2,1,0:T(8,128)(2,1)S(1)} %get-tuple-element.37), channel_id=1, source_target_pairs={{0,3},{1,2},{2,1},{3,0},{4,7},{5,6},{6,5},{7,4},{8,11},{9,10},{10,... | collective-permute-start | bytes 1572872 | tf_op jit(solution)/shard_map/ppermute | solution.py:315
  93.8 24.4 %collective-permute-start.7 = (bf16[256,8,128]{2,1,0:T(8,128)(2,1)S(1)}, bf16[256,8,128]{2,1,0:T(8,128)(2,1)S(1)}, u32[]{:S(2)}, u32[]{:S(2)}) collective-permute-start(bf16[256,8,128]{2,1,0:T(8,128)(2,1)S(1)} %get-tuple-element.38), channel_id=1, source_target_pairs={{0,1},{1,0},{2,3},{3,2},{4,5},{5,4},{6,7},{7,6},{8,9},{9,8},{10,11... | collective-permute-start | bytes 1572872 | tf_op jit(solution)/shard_map/ppermute | solution.py:315
  99.1 41.6 %collective-permute-start.5 = (bf16[256,8,128]{2,1,0:T(8,128)(2,1)S(1)}, bf16[256,8,128]{2,1,0:T(8,128)(2,1)S(1)}, u32[]{:S(2)}, u32[]{:S(2)}) collective-permute-start(bf16[256,8,128]{2,1,0:T(8,128)(2,1)S(1)} %get-tuple-element.36), channel_id=1, source_target_pairs={{0,2},{1,3},{2,0},{3,1},{4,6},{5,7},{6,4},{7,5},{8,10},{9,11},{10,... | collective-permute-start | bytes 1572872 | tf_op jit(solution)/shard_map/ppermute | solution.py:315
  99.2 42.9 %collective-permute-start.15 = (f32[4,128,128]{2,1,0:T(8,128)S(1)}, f32[4,128,128]{2,1,0:T(8,128)S(1)}, u32[]{:S(2)}, u32[]{:S(2)}) collective-permute-start(f32[4,128,128]{2,1,0:T(8,128)S(1)} %convert_add_fusion.refs_1_), channel_id=1, source_target_pairs={{0,4},{4,0},{8,12},{12,8},{16,20},{20,16},{24,28},{28,24},{1,5},{5... | collective-permute-start | bytes 786440 | tf_op jit(solution)/shard_map/ppermute | solution.py:192
